TPU v7x, 32 devices: a whole 2x2x4 slice. The times are simulated.
32 devices in a mesh: groups: 2 (over y), wide: 4 (over z), narrow: 4 (over x, core).
Axes of the slice: x: 2, y: 2, z: 4, core: 2. Of those that a mesh axis runs over, the one named last changes fastest.
Arguments:
- residual: bfloat16 [512, 4096], P(('groups', 'wide')), parts along dimension 0, may hold values from -6 to 6
- query_rows: bfloat16 [512, 4096], P(('groups', 'wide'), 'narrow'), parts along dimension 0, may hold values from -160 to 160
- key_rows: bfloat16 [512, 4096], P(('groups', 'wide'), 'narrow'), parts along dimension 0, may hold values from -160 to 160
- value_rows: bfloat16 [512, 4096], P(('groups', 'wide'), 'narrow'), parts along dimension 0, may hold values from -6 to 6
- segment_ids: int32 [8, 64], P(('groups', 'wide')), parts along dimension 0, may hold values from 0 to 3, never falling along the last dimension, each value on 1 to 32 neighbouring positions
- o_weight: bfloat16 [4096, 4096], P('narrow', 'wide'), may hold values from -0.09375 to 0.09375
- norm_gain: float32 [4096], replicated, may hold values from 0.1 to 1.9
- w_gate: bfloat16 [32, 4096, 1024], P('wide', None, 'narrow'), may hold values from -0.09375 to 0.09375
- w_up: bfloat16 [32, 4096, 1024], P('wide', None, 'narrow'), may hold values from -0.09375 to 0.09375
- w_down: bfloat16 [32, 1024, 4096], P('wide', None, 'narrow'), may hold values from -0.1875 to 0.1875
- expert_ids: int32 [512, 8], P(('groups', 'wide')), parts along dimension 0, may hold values from 0 to 31, all different within a row; in each aligned block of 16 rows (0 to 15, 16 to 31, ...) at most 8 rows name the same one
- gate_weights: float32 [512, 8], P(('groups', 'wide')), parts along dimension 0, may hold values from 0.05 to 1
- target: bfloat16 [512, 4096], P(('groups', 'wide', 'narrow')), parts along dimension 0, may hold values from -6 to 6
Outputs:
- errors: float32 [512], P(('groups', 'wide', 'narrow')), parts along dimension 0
There are 2 independent parts, one for each index of `groups`. A program takes and returns all parts, laid end to end along the dimension named above; an argument that names none is the same for every part. Nothing has to cross between parts.
Inputs may be any that keep to these rules, and one draw needn't show every extreme that they name: `expert_ids`: in each aligned block of 16 rows (the rows of one device) no expert is named more than 8 times, a bound that some block reaches. `segment_ids`: along each row the trajectory number never falls; a trajectory covers 1 to 32 positions.
All inputs are finite; a program needn't handle non-finite values.
Results may differ from a plain program's by a relative error of at most 0.0005.
Values may be sent and summed in bfloat16 or wider, within the bound.
No kernel may reach another device: no remote copies, remote signals or barrier semaphores. Data moves between devices by JAX's collectives and lax.ppermute only.
A program may use at most 128 MiB of HBM per device.

v0:
```python
import functools

import jax
import jax.numpy as jnp
from jax import lax
from jax.experimental import pallas as pl
from jax.experimental.pallas import tpu as pltpu
from jax.sharding import PartitionSpec as P


HD = 128
EXPERTS = 32
TOP = 8
BF16 = jnp.bfloat16
F32 = jnp.float32
PARTS = 2


def whole(shape):
    rank = len(shape)
    return pl.BlockSpec(shape, lambda *_: (0,) * rank, pipeline_mode=pl.Buffered(1))


def dot(a, b, dims=((1,), (0,))):
    return lax.dot_general(a, b, (dims, ((), ())), preferred_element_type=F32)


def each(count, step):
    if count == 1:
        step(0)
    else:
        lax.fori_loop(0, count, lambda i, carry: (step(i), carry)[1], 0)


def chunk_of(total, most):
    return most if total % most == 0 else total


def wide_pieces(rows):
    count = lax.axis_size("wide")
    me = lax.axis_index("wide")
    if count > 8:
        return [lax.all_gather(rows, "wide", axis=0)], jnp.arange(count, dtype=jnp.int32)
    found = [rows[None]]
    for step in range(1, count):
        found.append(lax.ppermute(rows, "wide", [((i + step) % count, i) for i in range(count)])[None])
    return found, (me + jnp.arange(count, dtype=jnp.int32)) % count


def wide_exchange(block_of, after):
    count = lax.axis_size("wide")
    me = lax.axis_index("wide")
    if count > 8:
        stacked = jnp.stack([block_of(i) for i in range(count)])
        return [lax.all_to_all(stacked, "wide", split_axis=0, concat_axis=0, tiled=True)]
    found = [block_of(me)[None]]
    blocks, _ = lax.optimization_barrier(([block_of((me - step) % count) for step in range(1, count)], after))
    for step in range(1, count):
        pairs = [((i + step) % count, i) for i in range(count)]
        found.append(lax.ppermute(blocks[step - 1], "wide", pairs)[None])
    return found


def narrow_flip(rows, bit):
    count = lax.axis_size("narrow")
    return lax.ppermute(rows, "narrow", [(i, i ^ bit) for i in range(count)])


def narrow_pieces(rows, after=None):
    count = lax.axis_size("narrow")
    held = {0: rows}
    bit = count // 2
    while bit:
        for j in list(held):
            held[j ^ bit] = narrow_flip(held[j], bit)
        if after is not None and bit == count // 2:
            held[bit], after = lax.optimization_barrier((held[bit], after))
        bit //= 2
    return [held[j] for j in range(count)], after


def attend_kernel(q_ref, k_ref, v_ref, seg_ref, out_ref):
    tok_count, width = q_ref.shape
    seg = jnp.broadcast_to(seg_ref[...].astype(F32), (tok_count, tok_count))
    key_pos = lax.broadcasted_iota(jnp.int32, (tok_count, tok_count), 1)
    query_pos = lax.broadcasted_iota(jnp.int32, (tok_count, tok_count), 0)
    allowed = (seg == seg.T) & (key_pos <= query_pos)
    for h in range(width // HD):
        cols = slice(h * HD, (h + 1) * HD)
        scores = dot(q_ref[:, cols], k_ref[:, cols], ((1,), (1,))) * HD ** (-0.5)
        scores = jnp.where(allowed, scores, -jnp.inf)
        weights = jnp.exp(scores - jnp.max(scores, axis=1, keepdims=True))
        denom = jnp.sum(weights, axis=1, keepdims=True)
        out_ref[:, cols] = (dot(weights.astype(BF16), v_ref[:, cols]) / denom).astype(BF16)


def attend(q, k, v, seg):
    return pl.pallas_call(attend_kernel, out_shape=jax.ShapeDtypeStruct(q.shape, BF16), name="attend")(q, k, v, seg)


def project_kernel(place_ref, *refs, pieces, n_count):
    att, w_ref, outs, product_ref = refs[:pieces], refs[pieces], refs[pieces + 1 : -1], refs[-1]
    me = place_ref[0]
    rows = jnp.concatenate([a[i] for a in att for i in range(a.shape[0])], axis=0)
    product_ref[...] = dot(rows, w_ref[...]).reshape(product_ref.shape)

    def spread(i, carry):
        w = place_ref[1 + i]
        for j in range(n_count):
            outs[j][w] = product_ref[i, me ^ j].astype(outs[j].dtype)
        return carry

    lax.fori_loop(0, product_ref.shape[0], spread, 0)


def project(place, att, o_weight, n_count):
    w_count = sum(a.shape[0] for a in att)
    tok_count, width = att[0].shape[1], o_weight.shape[1]
    shape = (w_count, tok_count // n_count, width)
    outs = [jax.ShapeDtypeStruct(shape, F32 if j == 0 else BF16) for j in range(n_count)]
    return pl.pallas_call(
        functools.partial(project_kernel, pieces=len(att), n_count=n_count),
        grid_spec=pltpu.PrefetchScalarGridSpec(
            num_scalar_prefetch=1,
            grid=(1,),
            in_specs=[whole(a.shape) for a in att] + [whole(o_weight.shape)],
            out_specs=[whole(shape) for _ in outs],
            scratch_shapes=[pltpu.VMEM((w_count, n_count, *shape[1:]), F32)],
        ),
        out_shape=outs,
        name="project",
    )(place, *att, o_weight)


def stream_kernel(place_ref, gain_ref, *refs, parts, pieces):
    shares, resid, out_ref = refs[:parts], refs[parts : parts + pieces], refs[parts + pieces]
    index = 0
    for a in resid:
        for i in range(a.shape[0]):
            w = place_ref[1 + index]
            index += 1
            total = a[i].astype(F32)
            for s in shares:
                total = total + s[w].astype(F32)
            out_ref[w] = (total * gain_ref[...]).astype(BF16)


def stream_of(place, gain_here, shares, resid):
    shape = shares[0].shape
    return pl.pallas_call(
        functools.partial(stream_kernel, parts=len(shares), pieces=len(resid)),
        grid_spec=pltpu.PrefetchScalarGridSpec(
            num_scalar_prefetch=1,
            grid=(1,),
            in_specs=[whole(gain_here.shape)] + [whole(a.shape) for a in (*shares, *resid)],
            out_specs=whole(shape),
        ),
        out_shape=jax.ShapeDtypeStruct(shape, BF16),
        name="stream",
    )(place, gain_here, *shares, *resid)


def base_kernel(place_ref, gain_ref, target_ref, *refs):
    pieces, base_ref = refs[:-1], refs[-1]
    width = pieces[0].shape[2]
    part = target_ref.shape[0]
    for i, piece in enumerate(pieces):
        col = pl.multiple_of(place_ref[1 + i] * width, 128)
        own = piece[0, pl.ds(pl.multiple_of(place_ref[0] * part, 8), part), :].astype(F32)
        base_ref[:, pl.ds(col, width)] = own / gain_ref[:, pl.ds(col, width)] - target_ref[:, pl.ds(col, width)].astype(F32)


def base_of(place, gain, target, pieces):
    return pl.pallas_call(
        base_kernel,
        grid_spec=pltpu.PrefetchScalarGridSpec(
            num_scalar_prefetch=1,
            grid=(1,),
            in_specs=[whole(a.shape) for a in (gain, target, *pieces)],
            out_specs=whole(target.shape),
        ),
        out_shape=jax.ShapeDtypeStruct(target.shape, F32),
        name="base",
    )(place, gain, target, *pieces)


def hidden_kernel(place_ref, slot_ref, norm_ref, *refs, groups, first_call):
    total = sum(groups)
    pieces, wg_ref, wu_ref, out_ref = refs[:total], refs[total], refs[total + 1], refs[total + 2]
    rest = list(refs[total + 3 :])
    scale_ref = rest.pop(0) if first_call else norm_ref
    hidden_ref = rest.pop(0)
    tokens = scale_ref.shape[0]
    rows_ref = rest.pop(0) if total > 1 else pieces[0].at[0]
    model_width = wg_ref.shape[1]

    @pl.when(pl.program_id(0) == 0)
    def _():
        if total > 1:
            block, width = pieces[0].shape[1:]
            for i, count in enumerate(groups):
                col = pl.multiple_of(place_ref[1 + i] * width, 128)
                for j in range(count):
                    rows_ref[j * block : (j + 1) * block, pl.ds(col, width)] = pieces[i * count + j][0]
        if first_call:
            some = chunk_of(tokens, 64)
            wide = chunk_of(model_width, 1024)

            def scale_rows(c):
                here = pl.ds(pl.multiple_of(c * some, 16), some)
                sums = 0.0
                for first in range(0, model_width, wide):
                    inverse = 1.0 / norm_ref[:, first : first + wide]
                    stream = rows_ref[here, first : first + wide].astype(F32) * inverse
                    sums += jnp.sum(stream * stream, axis=1, keepdims=True)
                scale_ref[here, :] = jnp.broadcast_to(lax.rsqrt(sums / model_width + 1e-06), (some, 128))

            each(tokens // some, scale_rows)

    many = chunk_of(tokens, 256)

    def rows_done(c):
        here = pl.ds(pl.multiple_of(c * many, 128), many)
        rows = rows_ref[here, :]
        scale = scale_ref[here, :1]
        gate_val = dot(rows, wg_ref[0]) * scale
        up_val = dot(rows, wu_ref[0]) * scale
        hidden_ref[here, :] = (gate_val / (1.0 + jnp.exp(-gate_val)) * up_val).astype(BF16)

    each(tokens // many, rows_done)
    slots = out_ref.shape[1]
    few = chunk_of(slots, 128)

    def slots_done(c):
        first = pl.multiple_of(c * few, 16)
        slot = jnp.broadcast_to(slot_ref[0], (few, tokens))
        chosen = (lax.broadcasted_iota(jnp.int32, slot.shape, 0) + first == slot).astype(F32).astype(BF16)
        out_ref[0, pl.ds(first, few), :] = dot(chosen, hidden_ref[...]).astype(BF16)

    each(slots // few, slots_done)


def hidden_of(place, slot, norm, pieces, w_gate, w_up, slots, first, experts):
    model_width, hid = w_gate.shape[1:]
    flat = [p for group in pieces for p in group]
    tokens = slot.shape[2]
    weight = pl.BlockSpec((1, model_width, hid), lambda e, *_: (first + e, 0, 0))
    rows = [pltpu.VMEM((tokens, model_width), BF16)] if len(flat) > 1 else []
    out_specs = [pl.BlockSpec((1, slots, hid), lambda e, *_: (e, 0, 0))]
    out_shape = [jax.ShapeDtypeStruct((experts, slots, hid), BF16)]
    if first == 0:
        out_specs.append(whole((tokens, 128)))
        out_shape.append(jax.ShapeDtypeStruct((tokens, 128), F32))
    found = pl.pallas_call(
        functools.partial(hidden_kernel, groups=[len(g) for g in pieces], first_call=first == 0),
        grid_spec=pltpu.PrefetchScalarGridSpec(
            num_scalar_prefetch=1,
            grid=(experts,),
            in_specs=[pl.BlockSpec((1, 1, tokens), lambda e, *_: (first + e, 0, 0)), whole(norm.shape)]
            + [whole(p.shape) for p in flat]
            + [weight, weight],
            out_specs=out_specs,
            scratch_shapes=[pltpu.VMEM((tokens, hid), BF16)] + rows,
        ),
        out_shape=out_shape,
        name="hidden",
    )(place, slot, norm, *flat, w_gate, w_up)
    return found if first == 0 else (found[0], norm)


def combine_kernel(place_ref, slot_ref, gate_ref, *refs, n_count, started):
    hidden, weights, rest = refs[:n_count], refs[n_count : 2 * n_count], refs[2 * n_count :]
    out_ref, sum_ref, result_ref = rest[-3:]
    group, slots, _ = hidden[0].shape

    @pl.when(pl.program_id(0) == 0)
    def _():
        sum_ref[...] = rest[0][...] if started else jnp.zeros_like(sum_ref)

    few = chunk_of(slots, 128)
    for e in range(group):

        def slots_done(c, e=e):
            here = pl.ds(pl.multiple_of(c * few, 16), few)
            result = 0.0
            for j in range(n_count):
                result += dot(hidden[j][e, here, :], weights[j][e])
            result_ref[pl.ds(pl.multiple_of(e * slots + c * few, 16), few), :] = result.astype(BF16)

        each(slots // few, slots_done)
    tokens = sum_ref.shape[0]
    many = chunk_of(tokens, 256)

    def rows_done(c):
        here = pl.ds(pl.multiple_of(c * many, 128), many)
        weight = []
        for e in range(group):
            slot = jnp.broadcast_to(slot_ref[e, :, here], (slots, many))
            gate = jnp.broadcast_to(gate_ref[e, :, here], (slots, many))
            weight.append(jnp.where(lax.broadcasted_iota(jnp.int32, slot.shape, 0) == slot, gate, 0.0))
        weight = jnp.concatenate(weight, axis=0) if group > 1 else weight[0]
        high = weight.astype(BF16)
        low = (weight - high.astype(F32)).astype(BF16)
        result = result_ref[...]
        sum_ref[here, :] += dot(high, result, ((0,), (0,))) + dot(low, result, ((0,), (0,)))

    each(tokens // many, rows_done)

    @pl.when(pl.program_id(0) == pl.num_programs(0) - 1)
    def _():
        out_ref[...] = sum_ref[...].astype(out_ref.dtype)


def combine(place, slot, gate, hidden, w_down, first, so_far, out_type):
    n_count = len(hidden)
    experts, slots, hid = hidden[0].shape
    group = 2 if experts % 2 == 0 else 1
    start = first // group
    tokens, width = slot.shape[2], w_down.shape[2]
    row = pl.BlockSpec((group, 1, tokens), lambda e, *_: (start + e, 0, 0))
    extra = [] if so_far is None else [so_far]
    return pl.pallas_call(
        functools.partial(combine_kernel, n_count=n_count, started=bool(extra)),
        grid_spec=pltpu.PrefetchScalarGridSpec(
            num_scalar_prefetch=1,
            grid=(experts // group,),
            in_specs=[row, row]
            + [pl.BlockSpec((group, slots, hid), lambda e, *_: (e, 0, 0)) for _ in hidden]
            + [
                pl.BlockSpec((group, hid, width), lambda e, place, j=j: (start + e, place[0] ^ j, 0))
                for j in range(n_count)
            ]
            + [whole(x.shape) for x in extra],
            out_specs=whole((tokens, width)),
            scratch_shapes=[pltpu.VMEM((tokens, width), F32), pltpu.VMEM((group * slots, width), BF16)],
        ),
        out_shape=jax.ShapeDtypeStruct((tokens, width), out_type),
        name="combine",
    )(place, slot, gate, *hidden, *[w_down] * n_count, *extra)


def routing(idx, packed, experts):
    stacked = jnp.concatenate(packed, axis=0)
    stacked = jnp.zeros_like(stacked).at[idx].set(stacked) if len(packed) == 1 else roll_wide(stacked)
    ids = stacked[:, :TOP].transpose(1, 0, 2).reshape(TOP, -1)
    gates = stacked[:, TOP:].transpose(1, 0, 2).reshape(TOP, -1)
    first = (lax.axis_index("wide") * experts).astype(F32)
    names = first + jnp.arange(experts, dtype=F32)
    same = ids[None] == names[:, None, None]
    member = jnp.any(same, axis=1)
    gate = jnp.sum(jnp.where(same, gates[None], 0.0), axis=1)
    tokens = ids.shape[1]
    before = (jnp.arange(tokens)[:, None] < jnp.arange(tokens)[None, :]).astype(BF16)
    rank = dot(member.astype(BF16), before).astype(jnp.int32)
    return jnp.where(member, rank, -1), gate


def roll_wide(stacked):
    count = stacked.shape[0]
    me = lax.axis_index("wide")
    return lax.dynamic_slice_in_dim(jnp.concatenate([stacked, stacked], axis=0), (count - me) % count, count, 0)


def body(
    residual,
    query_rows,
    key_rows,
    value_rows,
    segment_ids,
    o_weight,
    norm_gain,
    w_gate,
    w_up,
    w_down,
    expert_ids,
    gate_weights,
    target,
):
    w_count = lax.axis_size("wide")
    n_count = lax.axis_size("narrow")
    w_here = lax.axis_index("wide")
    n_here = lax.axis_index("narrow")
    tok_count, model_width = residual.shape
    part = tok_count // n_count
    experts = w_gate.shape[0]
    capacity = max(2, 2 * part * TOP // EXPERTS)
    slots = w_count * n_count * capacity
    out_width = o_weight.shape[1]

    attended = attend(query_rows, key_rows, value_rows, segment_ids)
    att_pieces, w_index = wide_pieces(attended)
    n_place = jnp.concatenate([n_here[None].astype(jnp.int32), w_index])
    w_place = jnp.concatenate([w_here[None].astype(jnp.int32), w_index])

    packed = jnp.concatenate([expert_ids.astype(F32).T, gate_weights.T], axis=0)
    packed, _ = lax.optimization_barrier((packed, attended))
    packed_pieces, _ = wide_pieces(packed)
    slot, gate = routing(w_index, packed_pieces, experts)
    by_place = slot.reshape(experts, w_count, n_count, part)
    slot_near = jnp.stack(
        [lax.dynamic_index_in_dim(by_place, n_here ^ j, 2, keepdims=False) for j in range(n_count)], axis=1
    ).reshape(experts, 1, -1)
    gain_here = lax.dynamic_slice_in_dim(norm_gain, w_here * out_width, out_width, 0)[None]

    shares = project(n_place, att_pieces, o_weight, n_count)
    own_resid = lax.dynamic_slice_in_dim(residual, n_here * part, part, 0)
    resid_pieces = wide_exchange(lambda w: lax.dynamic_slice_in_dim(own_resid, w * out_width, out_width, 1), shares[0])
    shares = [shares[0]] + [narrow_flip(shares[j], j) for j in range(1, n_count)]
    scaled = stream_of(n_place, gain_here, shares, resid_pieces).reshape(w_count * part, out_width)

    wide_rows, _ = wide_pieces(scaled)
    pieces = [narrow_pieces(rows)[0] for rows in wide_rows]
    if len(pieces) == 1 and w_count > 1:
        rows = jnp.stack(pieces[0]).transpose(0, 2, 1, 3).reshape(1, -1, model_width)
        pieces = [[rows]]
        w_place = jnp.stack([w_here, jnp.zeros_like(w_here)]).astype(jnp.int32)
    some = experts // PARTS if experts % (2 * PARTS) == 0 else experts
    norm, rows_of = norm_gain[None], []
    for first in range(0, experts, some):
        mine, norm = hidden_of(w_place, slot_near, norm, pieces, w_gate, w_up, slots, first, some)
        rows_of.append(mine)
    own_pieces, _ = lax.optimization_barrier(([group[0] for group in pieces], rows_of[-1]))
    base = base_of(w_place, norm_gain[None], target, own_pieces)
    partial_sum = None
    for i in range(len(rows_of)):
        later = i + 1 < len(rows_of)
        found, after = narrow_pieces(rows_of[i], (partial_sum, rows_of[i + 1] if later else None))
        partial_sum = after[0]
        if later:
            rows_of[i + 1] = after[1]
        out_type = F32 if later else BF16
        partial_sum = combine(n_place, slot[:, None], gate[:, None], found, w_down, i * some, partial_sum, out_type)
    returned = lax.all_to_all(
        partial_sum.reshape(w_count * n_count, part, -1),
        ("wide", "narrow"),
        split_axis=0,
        concat_axis=0,
        tiled=True,
    ).reshape(w_count, n_count, part, -1)
    moe_sum = jnp.sum(returned.astype(F32), axis=0).transpose(1, 0, 2)
    miss = base.reshape(moe_sum.shape) + moe_sum
    return jnp.sum(miss * miss, axis=(1, 2)) / model_width


def solution(mesh):
    return jax.shard_map(
        body,
        mesh=mesh,
        in_specs=(
            P(("groups", "wide"), None),
            P(("groups", "wide"), "narrow"),
            P(("groups", "wide"), "narrow"),
            P(("groups", "wide"), "narrow"),
            P(("groups", "wide"), None),
            P("narrow", "wide"),
            P(),
            P("wide", None, "narrow"),
            P("wide", None, "narrow"),
            P("wide", None, "narrow"),
            P(("groups", "wide"), None),
            P(("groups", "wide"), None),
            P(("groups", "wide", "narrow"), None),
        ),
        out_specs=P(("groups", "wide", "narrow")),
        check_vma=False,
    )
```

profile of v0, /device:TPU:0, one launch (start us, length us, event | category | flops | bytes accessed | tf_op | source)
XLA Modules:
  0.0 136.4 jit_solution(11468740103706515449)
XLA Ops:
  1.4 3.6 %attend.1 = bf16[64,1024]{1,0:T(8,128)(2,1)} custom-call(bf16[64,1024]{1,0:T(8,128)(2,1)} %q_ref.1, bf16[64,1024]{1,0:T(8,128)(2,1)} %k_ref.1, bf16[64,1024]{1,0:T(8,128)(2,1)} %v_ref.1, s32[1,64]{1,0:T(1,128)} %seg_ref.1), custom_call_target="tpu_custom_call" | custom-call | tf_op jit(solution)/shard_map/attend/pallas_call | solution.py:98
  4.9 3.1 %collective-permute-start.14 = (f32[16,64]{1,0:T(8,128)S(1)}, f32[16,64]{1,0:T(8,128)S(1)}, u32[]{:S(2)}, u32[]{:S(2)}) collective-permute-start(f32[16,64]{1,0:T(8,128)S(1)} %pad_maximum_fusion), channel_id=1, source_target_pairs={{12,0},{0,4},{4,8},{8,12},{13,1},{1,5},{5,9},{9,13},{14,2},{2,6},{... | collective-permute-start | bytes 12296 | tf_op jit(solution)/shard_map/ppermute | solution.py:46
  8.0 2.6 %collective-permute-start.13 = (f32[16,64]{1,0:T(8,128)S(1)}, f32[16,64]{1,0:T(8,128)S(1)}, u32[]{:S(2)}, u32[]{:S(2)}) collective-permute-start(f32[16,64]{1,0:T(8,128)S(1)} %pad_maximum_fusion), channel_id=1, source_target_pairs={{8,0},{12,4},{0,8},{4,12},{9,1},{13,5},{1,9},{5,13},{10,2},{14,6},... | collective-permute-start | bytes 12296 | tf_op jit(solution)/shard_map/ppermute | solution.py:46
  10.6 1.3 collective-permute-start.12
  13.6 1.6 %fusion.5 = (bf16[16,1024]{1,0:T(8,128)(2,1)S(1)}, bf16[16,1024]{1,0:T(8,128)(2,1)S(1)}, bf16[1,16,1024]{2,1,0:T(8,128)(2,1)}, bf16[16,1024]{1,0:T(8,128)(2,1)S(1)}) fusion(bf16[64,4096]{1,0:T(8,128)(2,1)} %param.13, s32[]{:T(128)S(6)} %select_n.78, s32[]{:T(128)S(6)} %select_n.88, s32[]{:T(128)S(6)} %select_n.82, s32[]{:T(128)S(6)} %select_n.79, ...), kind=kLoop, calls=%fused_computation.36 | loop fusion | bytes 262164 | tf_op jit(solution)/shard_map/dynamic_slice | solution.py:407
  16.5 2.8 %collective-permute-start = (bf16[64,1024]{1,0:T(8,128)(2,1)}, bf16[64,1024]{1,0:T(8,128)(2,1)S(1)}, u32[]{:S(2)}, u32[]{:S(2)}) collective-permute-start(bf16[64,1024]{1,0:T(8,128)(2,1)} %attend.1), channel_id=1, source_target_pairs={{4,0},{8,4},{12,8},{0,12},{5,1},{9,5},{13,9},{1,13},{6,2},{10,6},{... | collective-permute-start | bytes 393224 | tf_op jit(solution)/shard_map/ppermute | solution.py:46
  19.9 4.2 %collective-permute-done.1 = bf16[64,1024]{1,0:T(8,128)(2,1)S(1)} collective-permute-done((bf16[64,1024]{1,0:T(8,128)(2,1)}, bf16[64,1024]{1,0:T(8,128)(2,1)S(1)}, u32[]{:S(2)}, u32[]{:S(2)}) %collective-permute-start.1) | collective-permute-done | bytes 131104 | tf_op jit(solution)/shard_map/ppermute | solution.py:46
  25.5 4.2 %project.1 = (f32[4,16,1024]{2,1,0:T(8,128)}, bf16[4,16,1024]{2,1,0:T(8,128)(2,1)}, bf16[4,16,1024]{2,1,0:T(8,128)(2,1)}, bf16[4,16,1024]{2,1,0:T(8,128)(2,1)}) custom-call(s32[5]{0:T(128)} %get-tuple-element.51.place_ref, bf16[1,64,1024]{2,1,0:T(8,128)(2,1)} %bitcast.80, bf16[1,64,1024]{2,1,0:T(8,128)(2,1)} %bitcast.83, bf16[1,64,1024]{2,1,0:T(8,128)(2,1)} %bitcast.82, ...), custom_call_target="tpu_custom_call" | custom-call | tf_op jit(solution)/shard_map/project/pallas_call | solution.py:121
  29.7 1.8 %collective-permute-start.6 = (bf16[16,1024]{1,0:T(8,128)(2,1)S(1)}, bf16[16,1024]{1,0:T(8,128)(2,1)S(1)}, u32[]{:S(2)}, u32[]{:S(2)}) collective-permute-start(bf16[16,1024]{1,0:T(8,128)(2,1)S(1)} %get-tuple-element.27), channel_id=1, source_target_pairs={{4,0},{8,4},{12,8},{0,12},{5,1},{9,5},{13,9},{1,13},{6,2},{10,6},{... | collective-permute-start | bytes 98312 | tf_op jit(solution)/shard_map/ppermute | solution.py:60
  31.5 1.6 %collective-permute-start.7 = (bf16[16,1024]{1,0:T(8,128)(2,1)S(1)}, bf16[16,1024]{1,0:T(8,128)(2,1)S(1)}, u32[]{:S(2)}, u32[]{:S(2)}) collective-permute-start(bf16[16,1024]{1,0:T(8,128)(2,1)S(1)} %get-tuple-element.28), channel_id=1, source_target_pairs={{8,0},{12,4},{0,8},{4,12},{9,1},{13,5},{1,9},{5,13},{10,2},{14,6},... | collective-permute-start | bytes 98312 | tf_op jit(solution)/shard_map/ppermute | solution.py:60
  33.1 1.5 %collective-permute-start.4 = (bf16[4,16,1024]{2,1,0:T(8,128)(2,1)}, bf16[4,16,1024]{2,1,0:T(8,128)(2,1)S(1)}, u32[]{:S(2)}, u32[]{:S(2)}) collective-permute-start(bf16[4,16,1024]{2,1,0:T(8,128)(2,1)} %get-tuple-element.25), channel_id=1, source_target_pairs={{0,2},{1,3},{2,0},{3,1},{4,6},{5,7},{6,4},{7,5},{8,10},{9,11},{10,... | collective-permute-start | bytes 393224 | tf_op jit(solution)/shard_map/ppermute | solution.py:66
  35.0 1.3 collective-permute-done.7
  36.3 2.5 %collective-permute-done.8 = bf16[16,1024]{1,0:T(8,128)(2,1)S(1)} collective-permute-done((bf16[16,1024]{1,0:T(8,128)(2,1)S(1)}, bf16[16,1024]{1,0:T(8,128)(2,1)S(1)}, u32[]{:S(2)}, u32[]{:S(2)}) %collective-permute-start.8) | collective-permute-done | bytes 32800 | tf_op jit(solution)/shard_map/ppermute | solution.py:60
  39.7 1.9 %collective-permute-done.5.refs_3_ = bf16[4,16,1024]{2,1,0:T(8,128)(2,1)S(1)} collective-permute-done((bf16[4,16,1024]{2,1,0:T(8,128)(2,1)}, bf16[4,16,1024]{2,1,0:T(8,128)(2,1)S(1)}, u32[]{:S(2)}, u32[]{:S(2)}) %collective-permute-start.5) | collective-permute-done | bytes 131104 | tf_op jit(solution)/shard_map/ppermute | solution.py:66
  42.2 2.5 %stream.1 = bf16[4,16,1024]{2,1,0:T(8,128)(2,1)} custom-call(s32[5]{0:T(128)} %get-tuple-element.51.place_ref, f32[1,1024]{1,0:T(1,128)} %bitcast.93, f32[4,16,1024]{2,1,0:T(8,128)} %get-tuple-element.23.refs_0_, bf16[4,16,1024]{2,1,0:T(8,128)(2,1)} %copy-done.23, bf16[4,16,1024]{2,1,0:T(8,128)(2,1)} %copy-done.24, bf16[4,16,1024]{2,1,0:T(8,128)(2,1)} %copy-done.26, ...), custom_call_target="tpu_custom_call" | custom-call | tf_op jit(solution)/shard_map/stream/pallas_call | solution.py:150
  44.8 1.9 %collective-permute-start.11 = (bf16[64,1024]{1,0:T(8,128)(2,1)}, bf16[64,1024]{1,0:T(8,128)(2,1)S(1)}, u32[]{:S(2)}, u32[]{:S(2)}) collective-permute-start(bf16[64,1024]{1,0:T(8,128)(2,1)} %bitcast.54), channel_id=1, source_target_pairs={{12,0},{0,4},{4,8},{8,12},{13,1},{1,5},{5,9},{9,13},{14,2},{2,6},{... | collective-permute-start | bytes 393224 | tf_op jit(solution)/shard_map/ppermute | solution.py:46
  46.7 2.5 %collective-permute-start.10 = (bf16[64,1024]{1,0:T(8,128)(2,1)}, bf16[64,1024]{1,0:T(8,128)(2,1)S(1)}, u32[]{:S(2)}, u32[]{:S(2)}) collective-permute-start(bf16[64,1024]{1,0:T(8,128)(2,1)} %bitcast.55), channel_id=1, source_target_pairs={{8,0},{12,4},{0,8},{4,12},{9,1},{13,5},{1,9},{5,13},{10,2},{14,6},... | collective-permute-start | bytes 393224 | tf_op jit(solution)/shard_map/ppermute | solution.py:46
  49.2 1.5 %collective-permute-start.16 = (bf16[1,64,1024]{2,1,0:T(8,128)(2,1)}, bf16[1,64,1024]{2,1,0:T(8,128)(2,1)S(1)}, u32[]{:S(2)}, u32[]{:S(2)}) collective-permute-start(bf16[1,64,1024]{2,1,0:T(8,128)(2,1)} %bitcast.57), channel_id=1, source_target_pairs={{0,2},{1,3},{2,0},{3,1},{4,6},{5,7},{6,4},{7,5},{8,10},{9,11},{10,... | collective-permute-start | bytes 393224 | tf_op jit(solution)/shard_map/ppermute | solution.py:66
  50.9 2.3 %collective-permute-done.11 = bf16[64,1024]{1,0:T(8,128)(2,1)S(1)} collective-permute-done((bf16[64,1024]{1,0:T(8,128)(2,1)}, bf16[64,1024]{1,0:T(8,128)(2,1)S(1)}, u32[]{:S(2)}, u32[]{:S(2)}) %collective-permute-start.11) | collective-permute-done | bytes 131104 | tf_op jit(solution)/shard_map/ppermute | solution.py:46
  53.3 1.5 %collective-permute-start.25 = (bf16[1,64,1024]{2,1,0:T(8,128)(2,1)S(1)}, bf16[1,64,1024]{2,1,0:T(8,128)(2,1)S(1)}, u32[]{:S(2)}, u32[]{:S(2)}) collective-permute-start(bf16[1,64,1024]{2,1,0:T(8,128)(2,1)S(1)} %bitcast.64), channel_id=1, source_target_pairs={{0,2},{1,3},{2,0},{3,1},{4,6},{5,7},{6,4},{7,5},{8,10},{9,11},{10,... | collective-permute-start | bytes 393224 | tf_op jit(solution)/shard_map/ppermute | solution.py:66
  54.8 3.7 %collective-permute-done.10 = bf16[64,1024]{1,0:T(8,128)(2,1)S(1)} collective-permute-done((bf16[64,1024]{1,0:T(8,128)(2,1)}, bf16[64,1024]{1,0:T(8,128)(2,1)S(1)}, u32[]{:S(2)}, u32[]{:S(2)}) %collective-permute-start.10) | collective-permute-done | bytes 131104 | tf_op jit(solution)/shard_map/ppermute | solution.py:46
  58.5 1.6 %collective-permute-start.22 = (bf16[1,64,1024]{2,1,0:T(8,128)(2,1)S(1)}, bf16[1,64,1024]{2,1,0:T(8,128)(2,1)S(1)}, u32[]{:S(2)}, u32[]{:S(2)}) collective-permute-start(bf16[1,64,1024]{2,1,0:T(8,128)(2,1)S(1)} %bitcast.69), channel_id=1, source_target_pairs={{0,2},{1,3},{2,0},{3,1},{4,6},{5,7},{6,4},{7,5},{8,10},{9,11},{10,... | collective-permute-start | bytes 393224 | tf_op jit(solution)/shard_map/ppermute | solution.py:66
  61.6 3.3 %collective-permute-done.22.refs_10_ = bf16[1,64,1024]{2,1,0:T(8,128)(2,1)S(1)} collective-permute-done((bf16[1,64,1024]{2,1,0:T(8,128)(2,1)S(1)}, bf16[1,64,1024]{2,1,0:T(8,128)(2,1)S(1)}, u32[]{:S(2)}, u32[]{:S(2)}) %collective-permute-start.22) | collective-permute-done | bytes 131104 | tf_op jit(solution)/shard_map/ppermute | solution.py:66
  65.4 1.8 %collective-permute-done.19.refs_6_ = bf16[1,64,1024]{2,1,0:T(8,128)(2,1)S(1)} collective-permute-done((bf16[1,64,1024]{2,1,0:T(8,128)(2,1)S(1)}, bf16[1,64,1024]{2,1,0:T(8,128)(2,1)S(1)}, u32[]{:S(2)}, u32[]{:S(2)}) %collective-permute-start.19) | collective-permute-done | bytes 131104 | tf_op jit(solution)/shard_map/ppermute | solution.py:66
  69.2 12.4 %hidden.2 = (bf16[4,128,256]{2,1,0:T(8,128)(2,1)}, f32[256,128]{1,0:T(8,128)}) custom-call(s32[5]{0:T(128)} %get-tuple-element.52.place_ref, s32[8,1,256]{2,1,0:T(1,128)} %reshape.30.slot_ref, f32[1,4096]{1,0:T(1,128)} %bitcast.84, bf16[1,64,1024]{2,1,0:T(8,128)(2,1)} %bitcast.59, bf16[1,64,1024]{2,1,0:T(8,128)(2,1)} %copy-done.4, ...), custom_call_target="tpu_custom_call" | custom-call | tf_op jit(solution)/shard_map/hidden/pallas_call | solution.py:254
  81.6 1.5 %collective-permute-start.27 = (bf16[4,128,256]{2,1,0:T(8,128)(2,1)}, bf16[4,128,256]{2,1,0:T(8,128)(2,1)S(1)}, u32[]{:S(2)}, u32[]{:S(2)}) collective-permute-start(bf16[4,128,256]{2,1,0:T(8,128)(2,1)} %get-tuple-element.36.refs_0_), channel_id=1, source_target_pairs={{0,2},{1,3},{2,0},{3,1},{4,6},{5,7},{6,4},{7,5},{8,10},{9,11},{10,... | collective-permute-start | bytes 786440 | tf_op jit(solution)/shard_map/ppermute | solution.py:66
  83.2 11.6 %hidden.3.refs_0_ = bf16[4,128,256]{2,1,0:T(8,128)(2,1)} custom-call(s32[5]{0:T(128)} %get-tuple-element.52.place_ref, s32[8,1,256]{2,1,0:T(1,128)} %reshape.30.slot_ref, f32[256,128]{1,0:T(8,128)} %get-tuple-element.31.norm_ref, bf16[1,64,1024]{2,1,0:T(8,128)(2,1)} %bitcast.60, bf16[1,64,1024]{2,1,0:T(8,128)(2,1)} %copy-done.4, ...), custom_call_target="tpu_custom_call" | custom-call | tf_op jit(solution)/shard_map/hidden/pallas_call | solution.py:254
  98.7 6.7 %combine.2.refs_8_ = f32[256,1024]{1,0:T(8,128)} custom-call(s32[5]{0:T(128)} %get-tuple-element.51.place_ref, s32[8,1,256]{2,1,0:T(1,128)} %broadcast_in_dim.107.slot_ref, f32[8,1,256]{2,1,0:T(1,128)} %broadcast_in_dim.111.gate_ref, bf16[4,128,256]{2,1,0:T(8,128)(2,1)} %get-tuple-element.36.refs_0_, bf16[4,128,256]{2,1,0:T(8,128)(2,1)} %copy-done.16, ...), custom_call_target="tpu_custom_call" | custom-call | tf_op jit(solution)/shard_map/combine/pallas_call | solution.py:322
  107.9 6.8 %combine.3 = bf16[256,1024]{1,0:T(8,128)(2,1)} custom-call(s32[5]{0:T(128)} %get-tuple-element.51.place_ref, s32[8,1,256]{2,1,0:T(1,128)} %broadcast_in_dim.107.slot_ref, f32[8,1,256]{2,1,0:T(1,128)} %broadcast_in_dim.111.gate_ref, bf16[4,128,256]{2,1,0:T(8,128)(2,1)} %hidden.3.refs_0_, bf16[4,128,256]{2,1,0:T(8,128)(2,1)} %copy-done.19, ...), custom_call_target="tpu_custom_call" | custom-call | tf_op jit(solution)/shard_map/combine/pallas_call | solution.py:322
  114.7 5.7 %all-to-all-start = ((bf16[16,16,1024]{2,1,0:T(8,128)(2,1)}), bf16[16,16,1024]{2,1,0:T(8,128)(2,1)S(1)}, u32[]{:S(2)}, u32[]{:S(2)}) async-start(bf16[16,16,1024]{2,1,0:T(8,128)(2,1)} %bitcast.62), calls=%async_computation | async-start | bytes 1048576 | tf_op jit(solution)/shard_map/all_to_all | solution.py:433
  120.4 2.6 %base.1 = f32[16,4096]{1,0:T(8,128)} custom-call(s32[5]{0:T(128)} %get-tuple-element.52.place_ref, f32[1,4096]{1,0:T(1,128)} %bitcast.85, bf16[16,4096]{1,0:T(8,128)(2,1)} %target_ref.1, bf16[1,64,1024]{2,1,0:T(8,128)(2,1)} %bitcast.61, bf16[1,64,1024]{2,1,0:T(8,128)(2,1)} %bitcast.78, bf16[1,64,1024]{2,1,0:T(8,128)(2,1)} %bitcast.73, ...), custom_call_target="tpu_custom_call" | custom-call | tf_op jit(solution)/shard_map/base/pallas_call | solution.py:174
  123.0 11.7 %all-to-all-done = bf16[16,16,1024]{2,1,0:T(8,128)(2,1)S(1)} async-done(((bf16[16,16,1024]{2,1,0:T(8,128)(2,1)}), bf16[16,16,1024]{2,1,0:T(8,128)(2,1)S(1)}, u32[]{:S(2)}, u32[]{:S(2)}) %all-to-all-start) | async-done | bytes 524320 | tf_op jit(solution)/shard_map/all_to_all | solution.py:433
  (136 shorter events, 20.5 us)
Async XLA Ops:
  4.9 14.4 %collective-permute-start.14 = (f32[16,64]{1,0:T(8,128)S(1)}, f32[16,64]{1,0:T(8,128)S(1)}, u32[]{:S(2)}, u32[]{:S(2)}) collective-permute-start(f32[16,64]{1,0:T(8,128)S(1)} %pad_maximum_fusion), channel_id=1, source_target_pairs={{12,0},{0,4},{4,8},{8,12},{13,1},{1,5},{5,9},{9,13},{14,2},{2,6},{... | collective-permute-start | bytes 12296 | tf_op jit(solution)/shard_map/ppermute | solution.py:46
  8.0 11.3 %collective-permute-start.13 = (f32[16,64]{1,0:T(8,128)S(1)}, f32[16,64]{1,0:T(8,128)S(1)}, u32[]{:S(2)}, u32[]{:S(2)}) collective-permute-start(f32[16,64]{1,0:T(8,128)S(1)} %pad_maximum_fusion), channel_id=1, source_target_pairs={{8,0},{12,4},{0,8},{4,12},{9,1},{13,5},{1,9},{5,13},{10,2},{14,6},... | collective-permute-start | bytes 12296 | tf_op jit(solution)/shard_map/ppermute | solution.py:46
  10.6 5.9 %collective-permute-start.12 = (f32[16,64]{1,0:T(8,128)S(1)}, f32[16,64]{1,0:T(8,128)S(1)}, u32[]{:S(2)}, u32[]{:S(2)}) collective-permute-start(f32[16,64]{1,0:T(8,128)S(1)} %pad_maximum_fusion), channel_id=1, source_target_pairs={{4,0},{8,4},{12,8},{0,12},{5,1},{9,5},{13,9},{1,13},{6,2},{10,6},{... | collective-permute-start | bytes 12296 | tf_op jit(solution)/shard_map/ppermute | solution.py:46
  11.9 8.0 %collective-permute-start.2 = (bf16[64,1024]{1,0:T(8,128)(2,1)}, bf16[64,1024]{1,0:T(8,128)(2,1)S(1)}, u32[]{:S(2)}, u32[]{:S(2)}) collective-permute-start(bf16[64,1024]{1,0:T(8,128)(2,1)} %attend.1), channel_id=1, source_target_pairs={{12,0},{0,4},{4,8},{8,12},{13,1},{1,5},{5,9},{9,13},{14,2},{2,6},{... | collective-permute-start | bytes 393224 | tf_op jit(solution)/shard_map/ppermute | solution.py:46
  12.6 11.4 %collective-permute-start.1 = (bf16[64,1024]{1,0:T(8,128)(2,1)}, bf16[64,1024]{1,0:T(8,128)(2,1)S(1)}, u32[]{:S(2)}, u32[]{:S(2)}) collective-permute-start(bf16[64,1024]{1,0:T(8,128)(2,1)} %attend.1), channel_id=1, source_target_pairs={{8,0},{12,4},{0,8},{4,12},{9,1},{13,5},{1,9},{5,13},{10,2},{14,6},... | collective-permute-start | bytes 393224 | tf_op jit(solution)/shard_map/ppermute | solution.py:46
  16.5 8.3 %collective-permute-start = (bf16[64,1024]{1,0:T(8,128)(2,1)}, bf16[64,1024]{1,0:T(8,128)(2,1)S(1)}, u32[]{:S(2)}, u32[]{:S(2)}) collective-permute-start(bf16[64,1024]{1,0:T(8,128)(2,1)} %attend.1), channel_id=1, source_target_pairs={{4,0},{8,4},{12,8},{0,12},{5,1},{9,5},{13,9},{1,13},{6,2},{10,6},{... | collective-permute-start | bytes 393224 | tf_op jit(solution)/shard_map/ppermute | solution.py:46
  29.7 4.9 %collective-permute-start.6 = (bf16[16,1024]{1,0:T(8,128)(2,1)S(1)}, bf16[16,1024]{1,0:T(8,128)(2,1)S(1)}, u32[]{:S(2)}, u32[]{:S(2)}) collective-permute-start(bf16[16,1024]{1,0:T(8,128)(2,1)S(1)} %get-tuple-element.27), channel_id=1, source_target_pairs={{4,0},{8,4},{12,8},{0,12},{5,1},{9,5},{13,9},{1,13},{6,2},{10,6},{... | collective-permute-start | bytes 98312 | tf_op jit(solution)/shard_map/ppermute | solution.py:60
  31.5 4.8 %collective-permute-start.7 = (bf16[16,1024]{1,0:T(8,128)(2,1)S(1)}, bf16[16,1024]{1,0:T(8,128)(2,1)S(1)}, u32[]{:S(2)}, u32[]{:S(2)}) collective-permute-start(bf16[16,1024]{1,0:T(8,128)(2,1)S(1)} %get-tuple-element.28), channel_id=1, source_target_pairs={{8,0},{12,4},{0,8},{4,12},{9,1},{13,5},{1,9},{5,13},{10,2},{14,6},... | collective-permute-start | bytes 98312 | tf_op jit(solution)/shard_map/ppermute | solution.py:60
  33.1 5.7 %collective-permute-start.8 = (bf16[16,1024]{1,0:T(8,128)(2,1)S(1)}, bf16[16,1024]{1,0:T(8,128)(2,1)S(1)}, u32[]{:S(2)}, u32[]{:S(2)}) collective-permute-start(bf16[16,1024]{1,0:T(8,128)(2,1)S(1)} %get-tuple-element.29), channel_id=1, source_target_pairs={{12,0},{0,4},{4,8},{8,12},{13,1},{1,5},{5,9},{9,13},{14,2},{2,6},{... | collective-permute-start | bytes 98312 | tf_op jit(solution)/shard_map/ppermute | solution.py:60
  33.1 5.7 %collective-permute-start.3 = (bf16[4,16,1024]{2,1,0:T(8,128)(2,1)}, bf16[4,16,1024]{2,1,0:T(8,128)(2,1)S(1)}, u32[]{:S(2)}, u32[]{:S(2)}) collective-permute-start(bf16[4,16,1024]{2,1,0:T(8,128)(2,1)} %get-tuple-element.24), channel_id=1, source_target_pairs={{0,1},{1,0},{2,3},{3,2},{4,5},{5,4},{6,7},{7,6},{8,9},{9,8},{10,11... | collective-permute-start | bytes 393224 | tf_op jit(solution)/shard_map/ppermute | solution.py:66
  33.1 6.6 %collective-permute-start.4 = (bf16[4,16,1024]{2,1,0:T(8,128)(2,1)}, bf16[4,16,1024]{2,1,0:T(8,128)(2,1)S(1)}, u32[]{:S(2)}, u32[]{:S(2)}) collective-permute-start(bf16[4,16,1024]{2,1,0:T(8,128)(2,1)} %get-tuple-element.25), channel_id=1, source_target_pairs={{0,2},{1,3},{2,0},{3,1},{4,6},{5,7},{6,4},{7,5},{8,10},{9,11},{10,... | collective-permute-start | bytes 393224 | tf_op jit(solution)/shard_map/ppermute | solution.py:66
  34.6 7.0 %collective-permute-start.5 = (bf16[4,16,1024]{2,1,0:T(8,128)(2,1)}, bf16[4,16,1024]{2,1,0:T(8,128)(2,1)S(1)}, u32[]{:S(2)}, u32[]{:S(2)}) collective-permute-start(bf16[4,16,1024]{2,1,0:T(8,128)(2,1)} %get-tuple-element.26), channel_id=1, source_target_pairs={{0,3},{1,2},{2,1},{3,0},{4,7},{5,6},{6,5},{7,4},{8,11},{9,10},{10,... | collective-permute-start | bytes 393224 | tf_op jit(solution)/shard_map/ppermute | solution.py:66
  44.8 8.5 %collective-permute-start.11 = (bf16[64,1024]{1,0:T(8,128)(2,1)}, bf16[64,1024]{1,0:T(8,128)(2,1)S(1)}, u32[]{:S(2)}, u32[]{:S(2)}) collective-permute-start(bf16[64,1024]{1,0:T(8,128)(2,1)} %bitcast.54), channel_id=1, source_target_pairs={{12,0},{0,4},{4,8},{8,12},{13,1},{1,5},{5,9},{9,13},{14,2},{2,6},{... | collective-permute-start | bytes 393224 | tf_op jit(solution)/shard_map/ppermute | solution.py:46
  46.7 11.8 %collective-permute-start.10 = (bf16[64,1024]{1,0:T(8,128)(2,1)}, bf16[64,1024]{1,0:T(8,128)(2,1)S(1)}, u32[]{:S(2)}, u32[]{:S(2)}) collective-permute-start(bf16[64,1024]{1,0:T(8,128)(2,1)} %bitcast.55), channel_id=1, source_target_pairs={{8,0},{12,4},{0,8},{4,12},{9,1},{13,5},{1,9},{5,13},{10,2},{14,6},... | collective-permute-start | bytes 393224 | tf_op jit(solution)/shard_map/ppermute | solution.py:46
  49.2 9.3 %collective-permute-start.9 = (bf16[64,1024]{1,0:T(8,128)(2,1)}, bf16[64,1024]{1,0:T(8,128)(2,1)S(1)}, u32[]{:S(2)}, u32[]{:S(2)}) collective-permute-start(bf16[64,1024]{1,0:T(8,128)(2,1)} %bitcast.56), channel_id=1, source_target_pairs={{4,0},{8,4},{12,8},{0,12},{5,1},{9,5},{13,9},{1,13},{6,2},{10,6},{... | collective-permute-start | bytes 393224 | tf_op jit(solution)/shard_map/ppermute | solution.py:46
  49.2 10.8 %collective-permute-start.16 = (bf16[1,64,1024]{2,1,0:T(8,128)(2,1)}, bf16[1,64,1024]{2,1,0:T(8,128)(2,1)S(1)}, u32[]{:S(2)}, u32[]{:S(2)}) collective-permute-start(bf16[1,64,1024]{2,1,0:T(8,128)(2,1)} %bitcast.57), channel_id=1, source_target_pairs={{0,2},{1,3},{2,0},{3,1},{4,6},{5,7},{6,4},{7,5},{8,10},{9,11},{10,... | collective-permute-start | bytes 393224 | tf_op jit(solution)/shard_map/ppermute | solution.py:66
  50.7 9.5 %collective-permute-start.15 = (bf16[1,64,1024]{2,1,0:T(8,128)(2,1)}, bf16[1,64,1024]{2,1,0:T(8,128)(2,1)S(1)}, u32[]{:S(2)}, u32[]{:S(2)}) collective-permute-start(bf16[1,64,1024]{2,1,0:T(8,128)(2,1)} %bitcast.58), channel_id=1, source_target_pairs={{0,1},{1,0},{2,3},{3,2},{4,5},{5,4},{6,7},{7,6},{8,9},{9,8},{10,11... | collective-permute-start | bytes 393224 | tf_op jit(solution)/shard_map/ppermute | solution.py:66
  53.3 7.7 %collective-permute-start.25 = (bf16[1,64,1024]{2,1,0:T(8,128)(2,1)S(1)}, bf16[1,64,1024]{2,1,0:T(8,128)(2,1)S(1)}, u32[]{:S(2)}, u32[]{:S(2)}) collective-permute-start(bf16[1,64,1024]{2,1,0:T(8,128)(2,1)S(1)} %bitcast.64), channel_id=1, source_target_pairs={{0,2},{1,3},{2,0},{3,1},{4,6},{5,7},{6,4},{7,5},{8,10},{9,11},{10,... | collective-permute-start | bytes 393224 | tf_op jit(solution)/shard_map/ppermute | solution.py:66
  58.5 2.7 %collective-permute-start.24 = (bf16[1,64,1024]{2,1,0:T(8,128)(2,1)S(1)}, bf16[1,64,1024]{2,1,0:T(8,128)(2,1)S(1)}, u32[]{:S(2)}, u32[]{:S(2)}) collective-permute-start(bf16[1,64,1024]{2,1,0:T(8,128)(2,1)S(1)} %bitcast.65), channel_id=1, source_target_pairs={{0,1},{1,0},{2,3},{3,2},{4,5},{5,4},{6,7},{7,6},{8,9},{9,8},{10,11... | collective-permute-start | bytes 393224 | tf_op jit(solution)/shard_map/ppermute | solution.py:66
  58.5 6.4 %collective-permute-start.22 = (bf16[1,64,1024]{2,1,0:T(8,128)(2,1)S(1)}, bf16[1,64,1024]{2,1,0:T(8,128)(2,1)S(1)}, u32[]{:S(2)}, u32[]{:S(2)}) collective-permute-start(bf16[1,64,1024]{2,1,0:T(8,128)(2,1)S(1)} %bitcast.69), channel_id=1, source_target_pairs={{0,2},{1,3},{2,0},{3,1},{4,6},{5,7},{6,4},{7,5},{8,10},{9,11},{10,... | collective-permute-start | bytes 393224 | tf_op jit(solution)/shard_map/ppermute | solution.py:66
  60.0 4.9 %collective-permute-start.21 = (bf16[1,64,1024]{2,1,0:T(8,128)(2,1)S(1)}, bf16[1,64,1024]{2,1,0:T(8,128)(2,1)S(1)}, u32[]{:S(2)}, u32[]{:S(2)}) collective-permute-start(bf16[1,64,1024]{2,1,0:T(8,128)(2,1)S(1)} %bitcast.70), channel_id=1, source_target_pairs={{0,1},{1,0},{2,3},{3,2},{4,5},{5,4},{6,7},{7,6},{8,9},{9,8},{10,11... | collective-permute-start | bytes 393224 | tf_op jit(solution)/shard_map/ppermute | solution.py:66
  60.2 7.0 %collective-permute-start.19 = (bf16[1,64,1024]{2,1,0:T(8,128)(2,1)S(1)}, bf16[1,64,1024]{2,1,0:T(8,128)(2,1)S(1)}, u32[]{:S(2)}, u32[]{:S(2)}) collective-permute-start(bf16[1,64,1024]{2,1,0:T(8,128)(2,1)S(1)} %bitcast.74), channel_id=1, source_target_pairs={{0,2},{1,3},{2,0},{3,1},{4,6},{5,7},{6,4},{7,5},{8,10},{9,11},{10,... | collective-permute-start | bytes 393224 | tf_op jit(solution)/shard_map/ppermute | solution.py:66
  61.0 7.0 %collective-permute-start.18 = (bf16[1,64,1024]{2,1,0:T(8,128)(2,1)S(1)}, bf16[1,64,1024]{2,1,0:T(8,128)(2,1)S(1)}, u32[]{:S(2)}, u32[]{:S(2)}) collective-permute-start(bf16[1,64,1024]{2,1,0:T(8,128)(2,1)S(1)} %bitcast.75), channel_id=1, source_target_pairs={{0,1},{1,0},{2,3},{3,2},{4,5},{5,4},{6,7},{7,6},{8,9},{9,8},{10,11... | collective-permute-start | bytes 393224 | tf_op jit(solution)/shard_map/ppermute | solution.py:66
  61.2 6.8 %collective-permute-start.17 = (bf16[1,64,1024]{2,1,0:T(8,128)(2,1)S(1)}, bf16[1,64,1024]{2,1,0:T(8,128)(2,1)S(1)}, u32[]{:S(2)}, u32[]{:S(2)}) collective-permute-start(bf16[1,64,1024]{2,1,0:T(8,128)(2,1)S(1)} %collective-permute-done.16.refs_2_), channel_id=1, source_target_pairs={{0,1},{1,0},{2,3},{3,2},{4,5},{5,4},{6,7},{7,6},{8,9},{9,8},{10,11... | collective-permute-start | bytes 393224 | tf_op jit(solution)/shard_map/ppermute | solution.py:66
  64.9 3.1 %collective-permute-start.26 = (bf16[1,64,1024]{2,1,0:T(8,128)(2,1)S(1)}, bf16[1,64,1024]{2,1,0:T(8,128)(2,1)S(1)}, u32[]{:S(2)}, u32[]{:S(2)}) collective-permute-start(bf16[1,64,1024]{2,1,0:T(8,128)(2,1)S(1)} %collective-permute-done.25.refs_14_), channel_id=1, source_target_pairs={{0,1},{1,0},{2,3},{3,2},{4,5},{5,4},{6,7},{7,6},{8,9},{9,8},{10,11... | collective-permute-start | bytes 393224 | tf_op jit(solution)/shard_map/ppermute | solution.py:66
  64.9 3.1 %collective-permute-start.23 = (bf16[1,64,1024]{2,1,0:T(8,128)(2,1)S(1)}, bf16[1,64,1024]{2,1,0:T(8,128)(2,1)S(1)}, u32[]{:S(2)}, u32[]{:S(2)}) collective-permute-start(bf16[1,64,1024]{2,1,0:T(8,128)(2,1)S(1)} %collective-permute-done.22.refs_10_), channel_id=1, source_target_pairs={{0,1},{1,0},{2,3},{3,2},{4,5},{5,4},{6,7},{7,6},{8,9},{9,8},{10,11... | collective-permute-start | bytes 393224 | tf_op jit(solution)/shard_map/ppermute | solution.py:66
  81.6 13.1 %collective-permute-start.27 = (bf16[4,128,256]{2,1,0:T(8,128)(2,1)}, bf16[4,128,256]{2,1,0:T(8,128)(2,1)S(1)}, u32[]{:S(2)}, u32[]{:S(2)}) collective-permute-start(bf16[4,128,256]{2,1,0:T(8,128)(2,1)} %get-tuple-element.36.refs_0_), channel_id=1, source_target_pairs={{0,2},{1,3},{2,0},{3,1},{4,6},{5,7},{6,4},{7,5},{8,10},{9,11},{10,... | collective-permute-start | bytes 786440 | tf_op jit(solution)/shard_map/ppermute | solution.py:66
  83.2 14.1 %collective-permute-start.30 = (bf16[4,128,256]{2,1,0:T(8,128)(2,1)}, bf16[4,128,256]{2,1,0:T(8,128)(2,1)S(1)}, u32[]{:S(2)}, u32[]{:S(2)}) collective-permute-start(bf16[4,128,256]{2,1,0:T(8,128)(2,1)} %get-tuple-element.36.refs_0_), channel_id=1, source_target_pairs={{0,1},{1,0},{2,3},{3,2},{4,5},{5,4},{6,7},{7,6},{8,9},{9,8},{10,11... | collective-permute-start | bytes 786440 | tf_op jit(solution)/shard_map/ppermute | solution.py:66
  94.8 2.5 %collective-permute-start.31 = (bf16[4,128,256]{2,1,0:T(8,128)(2,1)S(1)}, bf16[4,128,256]{2,1,0:T(8,128)(2,1)S(1)}, u32[]{:S(2)}, u32[]{:S(2)}) collective-permute-start(bf16[4,128,256]{2,1,0:T(8,128)(2,1)S(1)} %collective-permute-done.27.refs_2_), channel_id=1, source_target_pairs={{0,1},{1,0},{2,3},{3,2},{4,5},{5,4},{6,7},{7,6},{8,9},{9,8},{10,11... | collective-permute-start | bytes 786440 | tf_op jit(solution)/shard_map/ppermute | solution.py:66
  95.3 10.1 %collective-permute-start.29 = (bf16[4,128,256]{2,1,0:T(8,128)(2,1)}, bf16[4,128,256]{2,1,0:T(8,128)(2,1)S(1)}, u32[]{:S(2)}, u32[]{:S(2)}) collective-permute-start(bf16[4,128,256]{2,1,0:T(8,128)(2,1)} %hidden.3.refs_0_), channel_id=1, source_target_pairs={{0,2},{1,3},{2,0},{3,1},{4,6},{5,7},{6,4},{7,5},{8,10},{9,11},{10,... | collective-permute-start | bytes 786440 | tf_op jit(solution)/shard_map/ppermute | solution.py:66
  97.3 8.8 %collective-permute-start.28 = (bf16[4,128,256]{2,1,0:T(8,128)(2,1)}, bf16[4,128,256]{2,1,0:T(8,128)(2,1)S(1)}, u32[]{:S(2)}, u32[]{:S(2)}) collective-permute-start(bf16[4,128,256]{2,1,0:T(8,128)(2,1)} %hidden.3.refs_0_), channel_id=1, source_target_pairs={{0,1},{1,0},{2,3},{3,2},{4,5},{5,4},{6,7},{7,6},{8,9},{9,8},{10,11... | collective-permute-start | bytes 786440 | tf_op jit(solution)/shard_map/ppermute | solution.py:66
  114.7 20.0 %all-to-all-start = ((bf16[16,16,1024]{2,1,0:T(8,128)(2,1)}), bf16[16,16,1024]{2,1,0:T(8,128)(2,1)S(1)}, u32[]{:S(2)}, u32[]{:S(2)}) async-start(bf16[16,16,1024]{2,1,0:T(8,128)(2,1)} %bitcast.62), calls=%async_computation | async-start | bytes 1048576 | tf_op jit(solution)/shard_map/all_to_all | solution.py:433
  (32 other events, 117.0 us)
where the time goes:
time: 137 us; the launch traced here: 136 us
  Pallas kernels  50.4 us (37%)
  waiting for transfers between devices  36.5 us (27%)
  starting transfers between devices  35.8 us (26%)
  local copies, waits for them, and re-layouts  9.18 us (7%)
  other arithmetic  3.94 us (3%)
    pallas_call x2, Pallas kernels, hidden_of(): pl.pallas_call(functools.partial(hidden_kernel, groups=[len(g) for g in p...  24 us
    ppermute x9, starting transfers between devices, wide_pieces(): lax.ppermute(rows, 'wide', [((i + step) % count, i) for i in range(count)])  15.3 us
    pallas_call x2, Pallas kernels, combine(): pl.pallas_call(functools.partial(combine_kernel, n_count=n_count, started...  13.5 us
    all_to_all x1, waiting for transfers between devices, body(): lax.all_to_all(partial_sum.reshape(w_count * n_count, part, -1), ('wide',...  11.7 us
    ppermute x9, waiting for transfers between devices, wide_pieces(): lax.ppermute(rows, 'wide', [((i + step) % count, i) for i in range(count)])  11.5 us
    ppermute x21, starting transfers between devices, narrow_flip(): return lax.ppermute(rows, 'narrow', [(i, i ^ bit) for i in range(count)])  11.4 us
    ppermute x21, waiting for transfers between devices, narrow_flip(): return lax.ppermute(rows, 'narrow', [(i, i ^ bit) for i in range(count)])  9.5 us
    all_to_all x1, starting transfers between devices, body(): lax.all_to_all(partial_sum.reshape(w_count * n_count, part, -1), ('wide',...  5.67 us
  transfers between devices with their start and end apart: 34, of which 14 were waited for; matrix products, arithmetic and copies ran while one was open for 5% of the time, Pallas kernels for 15%

commit v1 on v0

--- a/solution.py
+++ b/solution.py
@@ -1,4 +1,5 @@
 import functools
+import math
 
 import jax
 import jax.numpy as jnp
@@ -14,11 +15,18 @@
 BF16 = jnp.bfloat16
 F32 = jnp.float32
 PARTS = 2
+SPARE = 3 << 20
+STREAMED = 50 << 20
 
 
 def whole(shape):
     rank = len(shape)
     return pl.BlockSpec(shape, lambda *_: (0,) * rank, pipeline_mode=pl.Buffered(1))
+
+
+def room(*arrays, twice=(), least=0):
+    size = sum(a.size * a.dtype.itemsize for a in arrays) + 2 * sum(math.prod(n) * 2 for n in twice)
+    return pltpu.CompilerParams(vmem_limit_bytes=min(60 << 20, max(least, size + SPARE)))
 
 
 def dot(a, b, dims=((1,), (0,))):
@@ -95,7 +103,9 @@
 
 
 def attend(q, k, v, seg):
-    return pl.pallas_call(attend_kernel, out_shape=jax.ShapeDtypeStruct(q.shape, BF16), name="attend")(q, k, v, seg)
+    out_shape = jax.ShapeDtypeStruct(q.shape, BF16)
+    grant = room(q, k, v, out_shape)
+    return pl.pallas_call(attend_kernel, out_shape=out_shape, compiler_params=grant, name="attend")(q, k, v, seg)
 
 
 def project_kernel(place_ref, *refs, pieces, n_count):
@@ -128,6 +138,7 @@
             scratch_shapes=[pltpu.VMEM((w_count, n_count, *shape[1:]), F32)],
         ),
         out_shape=outs,
+        compiler_params=room(*att, o_weight, *outs, *outs, *outs),
         name="project",
     )(place, *att, o_weight)
 
@@ -156,6 +167,7 @@
             out_specs=whole(shape),
         ),
         out_shape=jax.ShapeDtypeStruct(shape, BF16),
+        compiler_params=room(*shares, *resid, shares[0]),
         name="stream",
     )(place, gain_here, *shares, *resid)
 
@@ -180,6 +192,7 @@
             out_specs=whole(target.shape),
         ),
         out_shape=jax.ShapeDtypeStruct(target.shape, F32),
+        compiler_params=room(*pieces, target, target, target),
         name="base",
     )(place, gain, target, *pieces)
 
@@ -198,10 +211,15 @@
     def _():
         if total > 1:
             block, width = pieces[0].shape[1:]
-            for i, count in enumerate(groups):
+            n_count, w_count = groups[0], len(groups)
+            part = block // w_count
+            for i in range(w_count):
                 col = pl.multiple_of(place_ref[1 + i] * width, 128)
-                for j in range(count):
-                    rows_ref[j * block : (j + 1) * block, pl.ds(col, width)] = pieces[i * count + j][0]
+                for k in range(w_count):
+                    source = pl.ds(pl.multiple_of(place_ref[1 + k] * part, part), part)
+                    for j in range(n_count):
+                        row = pl.multiple_of((k * n_count + (place_ref[0] ^ j)) * part, part)
+                        rows_ref[pl.ds(row, part), pl.ds(col, width)] = pieces[i * n_count + j][0, source, :]
         if first_call:
             some = chunk_of(tokens, 64)
             wide = chunk_of(model_width, 1024)
@@ -263,12 +281,15 @@
             scratch_shapes=[pltpu.VMEM((tokens, hid), BF16)] + rows,
         ),
         out_shape=out_shape,
+        compiler_params=room(
+            *flat, *flat, slot, slot, slot, twice=[(model_width, hid)] * 2 + [(slots, hid), (tokens, 4 * hid)], least=STREAMED
+        ),
         name="hidden",
     )(place, slot, norm, *flat, w_gate, w_up)
     return found if first == 0 else (found[0], norm)
 
 
-def combine_kernel(place_ref, slot_ref, gate_ref, *refs, n_count, started):
+def combine_kernel(place_ref, slot_ref, gate_ref, *refs, n_count, w_count, started):
     hidden, weights, rest = refs[:n_count], refs[n_count : 2 * n_count], refs[2 * n_count :]
     out_ref, sum_ref, result_ref = rest[-3:]
     group, slots, _ = hidden[0].shape
@@ -308,7 +329,13 @@
 
     @pl.when(pl.program_id(0) == pl.num_programs(0) - 1)
     def _():
-        out_ref[...] = sum_ref[...].astype(out_ref.dtype)
+        if out_ref.dtype == F32:
+            out_ref[...] = sum_ref[...]
+        else:
+            block = tokens // w_count
+            for k in range(w_count):
+                row = pl.multiple_of(place_ref[1 + k] * block, 16)
+                out_ref[pl.ds(row, block), :] = sum_ref[k * block : (k + 1) * block, :].astype(BF16)
 
 
 def combine(place, slot, gate, hidden, w_down, first, so_far, out_type):
@@ -320,7 +347,7 @@
     row = pl.BlockSpec((group, 1, tokens), lambda e, *_: (start + e, 0, 0))
     extra = [] if so_far is None else [so_far]
     return pl.pallas_call(
-        functools.partial(combine_kernel, n_count=n_count, started=bool(extra)),
+        functools.partial(combine_kernel, n_count=n_count, w_count=place.shape[0] - 1, started=bool(extra)),
         grid_spec=pltpu.PrefetchScalarGridSpec(
             num_scalar_prefetch=1,
             grid=(experts // group,),
@@ -335,30 +362,49 @@
             scratch_shapes=[pltpu.VMEM((tokens, width), F32), pltpu.VMEM((group * slots, width), BF16)],
         ),
         out_shape=jax.ShapeDtypeStruct((tokens, width), out_type),
+        compiler_params=room(
+            twice=[(group * hid * n_count, width), (group * n_count * slots, hid)] + [(tokens, width)] * 4
+            + [(group * slots, width)] * 2 + [(group * slots, chunk_of(tokens, 256))] * 4,
+            least=STREAMED,
+        ),
         name="combine",
     )(place, slot, gate, *hidden, *[w_down] * n_count, *extra)
 
 
-def routing(idx, packed, experts):
-    stacked = jnp.concatenate(packed, axis=0)
-    stacked = jnp.zeros_like(stacked).at[idx].set(stacked) if len(packed) == 1 else roll_wide(stacked)
-    ids = stacked[:, :TOP].transpose(1, 0, 2).reshape(TOP, -1)
-    gates = stacked[:, TOP:].transpose(1, 0, 2).reshape(TOP, -1)
-    first = (lax.axis_index("wide") * experts).astype(F32)
-    names = first + jnp.arange(experts, dtype=F32)
-    same = ids[None] == names[:, None, None]
-    member = jnp.any(same, axis=1)
-    gate = jnp.sum(jnp.where(same, gates[None], 0.0), axis=1)
-    tokens = ids.shape[1]
-    before = (jnp.arange(tokens)[:, None] < jnp.arange(tokens)[None, :]).astype(BF16)
-    rank = dot(member.astype(BF16), before).astype(jnp.int32)
-    return jnp.where(member, rank, -1), gate
-
-
-def roll_wide(stacked):
-    count = stacked.shape[0]
-    me = lax.axis_index("wide")
-    return lax.dynamic_slice_in_dim(jnp.concatenate([stacked, stacked], axis=0), (count - me) % count, count, 0)
+def route_kernel(place_ref, packed_ref, slot_ref, gate_ref):
+    experts, _, tokens = slot_ref.shape
+    ids, gates = packed_ref[:TOP, :], packed_ref[TOP:, :]
+    member = []
+    for e in range(experts):
+        same = ids == (place_ref[0] * experts + e).astype(F32)
+        member.append(jnp.max(same.astype(F32), axis=0, keepdims=True))
+        gate_ref[e] = jnp.sum(jnp.where(same, gates, 0.0), axis=0, keepdims=True)
+    member = jnp.concatenate(member, axis=0) if experts > 1 else member[0]
+    some = chunk_of(tokens, 256)
+    for first in range(0, tokens, some):
+        row = lax.broadcasted_iota(jnp.int32, (tokens, some), 0)
+        before = (row < lax.broadcasted_iota(jnp.int32, (tokens, some), 1) + first).astype(F32).astype(BF16)
+        rank = dot(member.astype(BF16), before)
+        found = jnp.where(member[:, first : first + some] > 0, rank, -1.0).astype(jnp.int32)
+        for e in range(experts):
+            slot_ref[e, :, first : first + some] = found[e : e + 1]
+
+
+def routing(place, packed, experts):
+    tokens = packed.shape[1]
+    out_shape = [jax.ShapeDtypeStruct((experts, 1, tokens), t) for t in (jnp.int32, F32)]
+    return pl.pallas_call(
+        route_kernel,
+        grid_spec=pltpu.PrefetchScalarGridSpec(
+            num_scalar_prefetch=1,
+            grid=(1,),
+            in_specs=[whole(packed.shape)],
+            out_specs=[whole(o.shape) for o in out_shape],
+        ),
+        out_shape=out_shape,
+        compiler_params=room(packed, *out_shape, twice=[(tokens, chunk_of(tokens, 256))] * 4),
+        name="route",
+    )(place, packed)
 
 
 def body(
@@ -395,32 +441,32 @@
     packed = jnp.concatenate([expert_ids.astype(F32).T, gate_weights.T], axis=0)
     packed, _ = lax.optimization_barrier((packed, attended))
     packed_pieces, _ = wide_pieces(packed)
-    slot, gate = routing(w_index, packed_pieces, experts)
-    by_place = slot.reshape(experts, w_count, n_count, part)
-    slot_near = jnp.stack(
-        [lax.dynamic_index_in_dim(by_place, n_here ^ j, 2, keepdims=False) for j in range(n_count)], axis=1
-    ).reshape(experts, 1, -1)
+    shares = project(n_place, att_pieces, o_weight, n_count)
+    packed_pieces, _ = lax.optimization_barrier((packed_pieces, shares[0]))
+    each_wide = [piece[i] for piece in packed_pieces for i in range(piece.shape[0])]
+    slot, gate = routing(w_place, jnp.concatenate(each_wide, axis=1), experts)
     gain_here = lax.dynamic_slice_in_dim(norm_gain, w_here * out_width, out_width, 0)[None]
-
-    shares = project(n_place, att_pieces, o_weight, n_count)
     own_resid = lax.dynamic_slice_in_dim(residual, n_here * part, part, 0)
     resid_pieces = wide_exchange(lambda w: lax.dynamic_slice_in_dim(own_resid, w * out_width, out_width, 1), shares[0])
     shares = [shares[0]] + [narrow_flip(shares[j], j) for j in range(1, n_count)]
+    shares, slot, gate = lax.optimization_barrier((shares, slot, gate))
     scaled = stream_of(n_place, gain_here, shares, resid_pieces).reshape(w_count * part, out_width)
 
     wide_rows, _ = wide_pieces(scaled)
     pieces = [narrow_pieces(rows)[0] for rows in wide_rows]
     if len(pieces) == 1 and w_count > 1:
-        rows = jnp.stack(pieces[0]).transpose(0, 2, 1, 3).reshape(1, -1, model_width)
-        pieces = [[rows]]
-        w_place = jnp.stack([w_here, jnp.zeros_like(w_here)]).astype(jnp.int32)
+        rows = jnp.stack(pieces[0])[n_here ^ jnp.arange(n_count)].reshape(n_count, w_count, w_count, part, -1)
+        pieces = [[rows.transpose(2, 0, 3, 1, 4).reshape(1, -1, model_width)]]
+        own_place = jnp.stack([w_here * n_count + n_here, jnp.zeros_like(w_here)]).astype(jnp.int32)
+    else:
+        own_place = w_place
     some = experts // PARTS if experts % (2 * PARTS) == 0 else experts
     norm, rows_of = norm_gain[None], []
     for first in range(0, experts, some):
-        mine, norm = hidden_of(w_place, slot_near, norm, pieces, w_gate, w_up, slots, first, some)
+        mine, norm = hidden_of(n_place, slot, norm, pieces, w_gate, w_up, slots, first, some)
         rows_of.append(mine)
     own_pieces, _ = lax.optimization_barrier(([group[0] for group in pieces], rows_of[-1]))
-    base = base_of(w_place, norm_gain[None], target, own_pieces)
+    base = base_of(own_place, norm_gain[None], target, own_pieces)
     partial_sum = None
     for i in range(len(rows_of)):
         later = i + 1 < len(rows_of)
@@ -429,7 +475,7 @@
         if later:
             rows_of[i + 1] = after[1]
         out_type = F32 if later else BF16
-        partial_sum = combine(n_place, slot[:, None], gate[:, None], found, w_down, i * some, partial_sum, out_type)
+        partial_sum = combine(n_place, slot, gate, found, w_down, i * some, partial_sum, out_type)
     returned = lax.all_to_all(
         partial_sum.reshape(w_count * n_count, part, -1),
         ("wide", "narrow"),

time: 137 us -> 122 us (0.89)
  Pallas kernels: 50.4 us -> 36.5 us
  waiting for transfers between devices: 36.5 us -> 41.4 us
  starting transfers between devices: 35.8 us -> 33.7 us
  local copies, waits for them, and re-layouts: 9.18 us -> 7.4 us
  other arithmetic: 3.94 us -> 2.3 us
    pallas_call x2, Pallas kernels: 24 us -> 20.1 us  [hidden_of(): pl.pallas_call(functools.partial(hidden_kernel, groups=[len(g) for g in p...]
    pallas_call x3 -> x4, Pallas kernels: 17.1 us -> 13.8 us  [the longest x2 11.3 us: combine(): pl.pallas_call(functools.partial(combine_kernel, n_count=n_count, w_count...]
    pallas_call x1, Pallas kernels: 4.17 us -> 1.34 us  [project(): pl.pallas_call(functools.partial(project_kernel, pieces=len(att), n_count...]
    pallas_call x1, Pallas kernels: 2.59 us -> 0.59 us  [base_of(): pl.pallas_call(base_kernel, grid_spec=pltpu.PrefetchScalarGridSpec(num_sc...]
    all_to_all x1, waiting for transfers between devices: 11.7 us -> 13.7 us  [body(): lax.all_to_all(partial_sum.reshape(w_count * n_count, part, -1), ('wide',...]
    pallas_call x1, Pallas kernels: 2.55 us -> 0.63 us  [stream_of(): pl.pallas_call(functools.partial(stream_kernel, parts=len(shares), pieces...]
    ppermute x21, starting transfers between devices: 11.4 us -> 9.65 us  [narrow_flip(): return lax.ppermute(rows, 'narrow', [(i, i ^ bit) for i in range(count)])]
    unnamed x67 -> x16, local copies, waits for them, and re-layouts: 4.05 us -> 5.69 us
  transfers between devices with their start and end apart: 34 -> 34, of which waited for: 14 -> 14; matrix products, arithmetic and copies ran while one was open for 5% -> 3% of each run, Pallas kernels for 15% -> 13%
where the time goes in v1:
time: 122 us
  waiting for transfers between devices  41.4 us (34%)
  Pallas kernels  36.5 us (30%)
  starting transfers between devices  33.7 us (28%)
  local copies, waits for them, and re-layouts  7.4 us (6%)
  other arithmetic  2.3 us (2%)
    pallas_call x2, Pallas kernels, hidden_of(): pl.pallas_call(functools.partial(hidden_kernel, groups=[len(g) for g in p...  20.1 us
    ppermute x9, starting transfers between devices, wide_pieces(): lax.ppermute(rows, 'wide', [((i + step) % count, i) for i in range(count)])  16.5 us
    all_to_all x1, waiting for transfers between devices, body(): lax.all_to_all(partial_sum.reshape(w_count * n_count, part, -1), ('wide',...  13.7 us
    ppermute x9, waiting for transfers between devices, wide_pieces(): lax.ppermute(rows, 'wide', [((i + step) % count, i) for i in range(count)])  12.4 us
    pallas_call x2, Pallas kernels, combine(): pl.pallas_call(functools.partial(combine_kernel, n_count=n_count, w_count...  11.3 us
    ppermute x21, waiting for transfers between devices, narrow_flip(): return lax.ppermute(rows, 'narrow', [(i, i ^ bit) for i in range(count)])  10.9 us
    ppermute x21, starting transfers between devices, narrow_flip(): return lax.ppermute(rows, 'narrow', [(i, i ^ bit) for i in range(count)])  9.65 us
    unnamed x16, local copies, waits for them, and re-layouts  5.69 us
  transfers between devices with their start and end apart: 34, of which 14 were waited for; matrix products, arithmetic and copies ran while one was open for 3% of the time, Pallas kernels for 13%

profile of v1, /device:TPU:0, one launch (start us, length us, event | category | flops | bytes accessed | tf_op | source)
XLA Modules:
  0.0 121.5 jit_solution(17700918303466975130)
XLA Ops:
  3.4 1.9 %attend.1 = bf16[64,1024]{1,0:T(8,128)(2,1)S(1)} custom-call(bf16[64,1024]{1,0:T(8,128)(2,1)S(1)} %copy-done.1, bf16[64,1024]{1,0:T(8,128)(2,1)S(1)} %copy-done.2, bf16[64,1024]{1,0:T(8,128)(2,1)S(1)} %copy-done.3, s32[1,64]{1,0:T(1,128)S(1)} %copy-done.7), custom_call_target="tpu_custom_call" | custom-call | tf_op jit(solution)/shard_map/attend/pallas_call | solution.py:108
  5.2 3.1 %collective-permute-start.2 = (bf16[64,1024]{1,0:T(8,128)(2,1)S(1)}, bf16[64,1024]{1,0:T(8,128)(2,1)S(1)}, u32[]{:S(2)}, u32[]{:S(2)}) collective-permute-start(bf16[64,1024]{1,0:T(8,128)(2,1)S(1)} %attend.1), channel_id=1, source_target_pairs={{12,0},{0,4},{4,8},{8,12},{13,1},{1,5},{5,9},{9,13},{14,2},{2,6},{... | collective-permute-start | bytes 393224 | tf_op jit(solution)/shard_map/ppermute | solution.py:54
  8.4 2.6 %collective-permute-start.1 = (bf16[64,1024]{1,0:T(8,128)(2,1)S(1)}, bf16[64,1024]{1,0:T(8,128)(2,1)S(1)}, u32[]{:S(2)}, u32[]{:S(2)}) collective-permute-start(bf16[64,1024]{1,0:T(8,128)(2,1)S(1)} %attend.1), channel_id=1, source_target_pairs={{8,0},{12,4},{0,8},{4,12},{9,1},{13,5},{1,9},{5,13},{10,2},{14,6},... | collective-permute-start | bytes 393224 | tf_op jit(solution)/shard_map/ppermute | solution.py:54
  10.9 1.3 %collective-permute-start = (bf16[64,1024]{1,0:T(8,128)(2,1)S(1)}, bf16[64,1024]{1,0:T(8,128)(2,1)S(1)}, u32[]{:S(2)}, u32[]{:S(2)}) collective-permute-start(bf16[64,1024]{1,0:T(8,128)(2,1)S(1)} %attend.1), channel_id=1, source_target_pairs={{4,0},{8,4},{12,8},{0,12},{5,1},{9,5},{13,9},{1,13},{6,2},{10,6},{... | collective-permute-start | bytes 393224 | tf_op jit(solution)/shard_map/ppermute | solution.py:54
  13.1 1.8 %collective-permute-done.2 = bf16[64,1024]{1,0:T(8,128)(2,1)S(1)} collective-permute-done((bf16[64,1024]{1,0:T(8,128)(2,1)S(1)}, bf16[64,1024]{1,0:T(8,128)(2,1)S(1)}, u32[]{:S(2)}, u32[]{:S(2)}) %collective-permute-start.2) | collective-permute-done | bytes 131104 | tf_op jit(solution)/shard_map/ppermute | solution.py:54
  14.8 4.8 %collective-permute-done.1 = bf16[64,1024]{1,0:T(8,128)(2,1)S(1)} collective-permute-done((bf16[64,1024]{1,0:T(8,128)(2,1)S(1)}, bf16[64,1024]{1,0:T(8,128)(2,1)S(1)}, u32[]{:S(2)}, u32[]{:S(2)}) %collective-permute-start.1) | collective-permute-done | bytes 131104 | tf_op jit(solution)/shard_map/ppermute | solution.py:54
  19.6 1.6 %copy-done = bf16[1024,1024]{1,0:T(8,128)(2,1)S(1)} copy-done((bf16[1024,1024]{1,0:T(8,128)(2,1)S(1)}, bf16[1024,1024]{1,0:T(8,128)(2,1)}, u32[]{:S(2)}) %copy-start) | copy-done | bytes 2097176
  21.2 1.3 %project.1 = (f32[4,16,1024]{2,1,0:T(8,128)S(1)}, bf16[4,16,1024]{2,1,0:T(8,128)(2,1)S(1)}, bf16[4,16,1024]{2,1,0:T(8,128)(2,1)S(1)}, bf16[4,16,1024]{2,1,0:T(8,128)(2,1)S(1)}) custom-call(s32[5]{0:T(128)S(1)} %get-tuple-element.69.place_ref, bf16[1,64,1024]{2,1,0:T(8,128)(2,1)S(1)} %bitcast.65, bf16[1,64,1024]{2,1,0:T(8,128)(2,1)S(1)} %bitcast.68, ...), custom_call_target="tpu_custom_call" | custom-call | tf_op jit(solution)/shard_map/project/pallas_call | solution.py:131
  23.3 3.3 %collective-permute-start.8 = (f32[16,64]{1,0:T(8,128)S(1)}, f32[16,64]{1,0:T(8,128)S(1)}, u32[]{:S(2)}, u32[]{:S(2)}) collective-permute-start(f32[16,64]{1,0:T(8,128)S(1)} %pad_maximum_fusion.1), channel_id=1, source_target_pairs={{12,0},{0,4},{4,8},{8,12},{13,1},{1,5},{5,9},{9,13},{14,2},{2,6},{... | collective-permute-start | bytes 12296 | tf_op jit(solution)/shard_map/ppermute | solution.py:54
  26.6 1.6 %collective-permute-start.7 = (f32[16,64]{1,0:T(8,128)S(1)}, f32[16,64]{1,0:T(8,128)S(1)}, u32[]{:S(2)}, u32[]{:S(2)}) collective-permute-start(f32[16,64]{1,0:T(8,128)S(1)} %pad_maximum_fusion.1), channel_id=1, source_target_pairs={{8,0},{12,4},{0,8},{4,12},{9,1},{13,5},{1,9},{5,13},{10,2},{14,6},... | collective-permute-start | bytes 12296 | tf_op jit(solution)/shard_map/ppermute | solution.py:54
  28.9 1.5 %collective-permute-start.4 = (bf16[4,16,1024]{2,1,0:T(8,128)(2,1)S(1)}, bf16[4,16,1024]{2,1,0:T(8,128)(2,1)S(1)}, u32[]{:S(2)}, u32[]{:S(2)}) collective-permute-start(bf16[4,16,1024]{2,1,0:T(8,128)(2,1)S(1)} %get-tuple-element.37), channel_id=1, source_target_pairs={{0,2},{1,3},{2,0},{3,1},{4,6},{5,7},{6,4},{7,5},{8,10},{9,11},{10,... | collective-permute-start | bytes 393224 | tf_op jit(solution)/shard_map/ppermute | solution.py:74
  30.4 1.0 fusion.3
  32.2 2.2 %collective-permute-start.9 = (bf16[16,1024]{1,0:T(8,128)(2,1)S(1)}, bf16[16,1024]{1,0:T(8,128)(2,1)S(1)}, u32[]{:S(2)}, u32[]{:S(2)}) collective-permute-start(bf16[16,1024]{1,0:T(8,128)(2,1)S(1)} %get-tuple-element.50), channel_id=1, source_target_pairs={{4,0},{8,4},{12,8},{0,12},{5,1},{9,5},{13,9},{1,13},{6,2},{10,6},{... | collective-permute-start | bytes 98312 | tf_op jit(solution)/shard_map/ppermute | solution.py:68
  36.2 3.0 %collective-permute-done.10 = bf16[16,1024]{1,0:T(8,128)(2,1)S(1)} collective-permute-done((bf16[16,1024]{1,0:T(8,128)(2,1)S(1)}, bf16[16,1024]{1,0:T(8,128)(2,1)S(1)}, u32[]{:S(2)}, u32[]{:S(2)}) %collective-permute-start.10) | collective-permute-done | bytes 32800 | tf_op jit(solution)/shard_map/ppermute | solution.py:68
  39.2 1.4 %collective-permute-done.11 = bf16[16,1024]{1,0:T(8,128)(2,1)S(1)} collective-permute-done((bf16[16,1024]{1,0:T(8,128)(2,1)S(1)}, bf16[16,1024]{1,0:T(8,128)(2,1)S(1)}, u32[]{:S(2)}, u32[]{:S(2)}) %collective-permute-start.11) | collective-permute-done | bytes 32800 | tf_op jit(solution)/shard_map/ppermute | solution.py:68
  42.1 3.1 %collective-permute-start.12 = (bf16[64,1024]{1,0:T(8,128)(2,1)S(1)}, bf16[64,1024]{1,0:T(8,128)(2,1)S(1)}, u32[]{:S(2)}, u32[]{:S(2)}) collective-permute-start(bf16[64,1024]{1,0:T(8,128)(2,1)S(1)} %bitcast.43), channel_id=1, source_target_pairs={{4,0},{8,4},{12,8},{0,12},{5,1},{9,5},{13,9},{1,13},{6,2},{10,6},{... | collective-permute-start | bytes 393224 | tf_op jit(solution)/shard_map/ppermute | solution.py:54
  45.1 1.2 collective-permute-start.16
  46.3 3.2 %collective-permute-done.14 = bf16[64,1024]{1,0:T(8,128)(2,1)S(1)} collective-permute-done((bf16[64,1024]{1,0:T(8,128)(2,1)S(1)}, bf16[64,1024]{1,0:T(8,128)(2,1)S(1)}, u32[]{:S(2)}, u32[]{:S(2)}) %collective-permute-start.14) | collective-permute-done | bytes 131104 | tf_op jit(solution)/shard_map/ppermute | solution.py:54
  50.5 2.7 %collective-permute-done.13 = bf16[64,1024]{1,0:T(8,128)(2,1)S(1)} collective-permute-done((bf16[64,1024]{1,0:T(8,128)(2,1)S(1)}, bf16[64,1024]{1,0:T(8,128)(2,1)S(1)}, u32[]{:S(2)}, u32[]{:S(2)}) %collective-permute-start.13) | collective-permute-done | bytes 131104 | tf_op jit(solution)/shard_map/ppermute | solution.py:54
  53.2 1.4 %collective-permute-start.22 = (bf16[1,64,1024]{2,1,0:T(8,128)(2,1)S(1)}, bf16[1,64,1024]{2,1,0:T(8,128)(2,1)S(1)}, u32[]{:S(2)}, u32[]{:S(2)}) collective-permute-start(bf16[1,64,1024]{2,1,0:T(8,128)(2,1)S(1)} %bitcast.54), channel_id=1, source_target_pairs={{0,2},{1,3},{2,0},{3,1},{4,6},{5,7},{6,4},{7,5},{8,10},{9,11},{10,... | collective-permute-start | bytes 393224 | tf_op jit(solution)/shard_map/ppermute | solution.py:74
  56.0 3.6 %collective-permute-done.22.refs_10_ = bf16[1,64,1024]{2,1,0:T(8,128)(2,1)S(1)} collective-permute-done((bf16[1,64,1024]{2,1,0:T(8,128)(2,1)S(1)}, bf16[1,64,1024]{2,1,0:T(8,128)(2,1)S(1)}, u32[]{:S(2)}, u32[]{:S(2)}) %collective-permute-start.22) | collective-permute-done | bytes 131104 | tf_op jit(solution)/shard_map/ppermute | solution.py:74
  60.1 1.8 %collective-permute-done.19.refs_6_ = bf16[1,64,1024]{2,1,0:T(8,128)(2,1)S(1)} collective-permute-done((bf16[1,64,1024]{2,1,0:T(8,128)(2,1)S(1)}, bf16[1,64,1024]{2,1,0:T(8,128)(2,1)S(1)}, u32[]{:S(2)}, u32[]{:S(2)}) %collective-permute-start.19) | collective-permute-done | bytes 131104 | tf_op jit(solution)/shard_map/ppermute | solution.py:74
  62.0 1.3 %collective-permute-done.20.refs_7_ = bf16[1,64,1024]{2,1,0:T(8,128)(2,1)S(1)} collective-permute-done((bf16[1,64,1024]{2,1,0:T(8,128)(2,1)S(1)}, bf16[1,64,1024]{2,1,0:T(8,128)(2,1)S(1)}, u32[]{:S(2)}, u32[]{:S(2)}) %collective-permute-start.20) | collective-permute-done | bytes 131104 | tf_op jit(solution)/shard_map/ppermute | solution.py:74
  64.0 10.5 %hidden.2 = (bf16[4,128,256]{2,1,0:T(8,128)(2,1)S(1)}, f32[256,128]{1,0:T(8,128)S(1)}) custom-call(s32[5]{0:T(128)S(1)} %get-tuple-element.69.place_ref, s32[8,1,256]{2,1,0:T(1,128)S(1)} %get-tuple-element.53.slot_ref, f32[1,4096]{1,0:T(1,128)S(1)} %bitcast.69, bf16[1,64,1024]{2,1,0:T(8,128)(2,1)S(1)} %bitcast.46, ...), custom_call_target="tpu_custom_call" | custom-call | tf_op jit(solution)/shard_map/hidden/pallas_call | solution.py:272
  74.5 1.5 %collective-permute-start.27 = (bf16[4,128,256]{2,1,0:T(8,128)(2,1)S(1)}, bf16[4,128,256]{2,1,0:T(8,128)(2,1)S(1)}, u32[]{:S(2)}, u32[]{:S(2)}) collective-permute-start(bf16[4,128,256]{2,1,0:T(8,128)(2,1)S(1)} %get-tuple-element.60.refs_0_), channel_id=1, source_target_pairs={{0,2},{1,3},{2,0},{3,1},{4,6},{5,7},{6,4},{7,5},{8,10},{9,11},{10,... | collective-permute-start | bytes 786440 | tf_op jit(solution)/shard_map/ppermute | solution.py:74
  76.0 9.6 %hidden.3.refs_0_ = bf16[4,128,256]{2,1,0:T(8,128)(2,1)S(1)} custom-call(s32[5]{0:T(128)S(1)} %get-tuple-element.69.place_ref, s32[8,1,256]{2,1,0:T(1,128)S(1)} %get-tuple-element.53.slot_ref, f32[256,128]{1,0:T(8,128)S(1)} %get-tuple-element.54.norm_ref, bf16[1,64,1024]{2,1,0:T(8,128)(2,1)S(1)} %bitcast.47, ...), custom_call_target="tpu_custom_call" | custom-call | tf_op jit(solution)/shard_map/hidden/pallas_call | solution.py:272
  87.4 5.3 %combine.2.refs_8_ = f32[256,1024]{1,0:T(8,128)S(1)} custom-call(s32[5]{0:T(128)S(1)} %get-tuple-element.69.place_ref, s32[8,1,256]{2,1,0:T(1,128)S(1)} %get-tuple-element.53.slot_ref, f32[8,1,256]{2,1,0:T(1,128)S(1)} %get-tuple-element.59.gate_ref, bf16[4,128,256]{2,1,0:T(8,128)(2,1)S(1)} %get-tuple-element.60.refs_0_, ...), custom_call_target="tpu_custom_call" | custom-call | tf_op jit(solution)/shard_map/combine/pallas_call | solution.py:349
  92.7 1.8 %collective-permute-done.29.refs_2_ = bf16[4,128,256]{2,1,0:T(8,128)(2,1)S(1)} collective-permute-done((bf16[4,128,256]{2,1,0:T(8,128)(2,1)S(1)}, bf16[4,128,256]{2,1,0:T(8,128)(2,1)S(1)}, u32[]{:S(2)}, u32[]{:S(2)}) %collective-permute-start.29) | collective-permute-done | bytes 262176 | tf_op jit(solution)/shard_map/ppermute | solution.py:74
  94.5 1.5 %collective-permute-done.32.refs_3_ = bf16[4,128,256]{2,1,0:T(8,128)(2,1)S(1)} collective-permute-done((bf16[4,128,256]{2,1,0:T(8,128)(2,1)S(1)}, bf16[4,128,256]{2,1,0:T(8,128)(2,1)S(1)}, u32[]{:S(2)}, u32[]{:S(2)}) %collective-permute-start.32) | collective-permute-done | bytes 262176 | tf_op jit(solution)/shard_map/ppermute | solution.py:74
  96.0 6.0 %combine.3 = bf16[256,1024]{1,0:T(8,128)(2,1)} custom-call(s32[5]{0:T(128)S(1)} %get-tuple-element.69.place_ref, s32[8,1,256]{2,1,0:T(1,128)S(1)} %get-tuple-element.53.slot_ref, f32[8,1,256]{2,1,0:T(1,128)S(1)} %get-tuple-element.59.gate_ref, bf16[4,128,256]{2,1,0:T(8,128)(2,1)S(1)} %hidden.3.refs_0_, ...), custom_call_target="tpu_custom_call" | custom-call | tf_op jit(solution)/shard_map/combine/pallas_call | solution.py:349
  102.0 4.5 %all-to-all-start = ((bf16[16,16,1024]{2,1,0:T(8,128)(2,1)}), bf16[16,16,1024]{2,1,0:T(8,128)(2,1)S(1)}, u32[]{:S(2)}, u32[]{:S(2)}) async-start(bf16[16,16,1024]{2,1,0:T(8,128)(2,1)} %bitcast.27), calls=%async_computation | async-start | bytes 1048576 | tf_op jit(solution)/shard_map/all_to_all | solution.py:479
  107.1 13.7 %all-to-all-done = bf16[16,16,1024]{2,1,0:T(8,128)(2,1)S(1)} async-done(((bf16[16,16,1024]{2,1,0:T(8,128)(2,1)}), bf16[16,16,1024]{2,1,0:T(8,128)(2,1)S(1)}, u32[]{:S(2)}, u32[]{:S(2)}) %all-to-all-start) | async-done | bytes 524320 | tf_op jit(solution)/shard_map/all_to_all | solution.py:479
  (71 shorter events, 16.3 us)
Async XLA Ops:
  5.2 9.6 %collective-permute-start.2 = (bf16[64,1024]{1,0:T(8,128)(2,1)S(1)}, bf16[64,1024]{1,0:T(8,128)(2,1)S(1)}, u32[]{:S(2)}, u32[]{:S(2)}) collective-permute-start(bf16[64,1024]{1,0:T(8,128)(2,1)S(1)} %attend.1), channel_id=1, source_target_pairs={{12,0},{0,4},{4,8},{8,12},{13,1},{1,5},{5,9},{9,13},{14,2},{2,6},{... | collective-permute-start | bytes 393224 | tf_op jit(solution)/shard_map/ppermute | solution.py:54
  8.4 11.2 %collective-permute-start.1 = (bf16[64,1024]{1,0:T(8,128)(2,1)S(1)}, bf16[64,1024]{1,0:T(8,128)(2,1)S(1)}, u32[]{:S(2)}, u32[]{:S(2)}) collective-permute-start(bf16[64,1024]{1,0:T(8,128)(2,1)S(1)} %attend.1), channel_id=1, source_target_pairs={{8,0},{12,4},{0,8},{4,12},{9,1},{13,5},{1,9},{5,13},{10,2},{14,6},... | collective-permute-start | bytes 393224 | tf_op jit(solution)/shard_map/ppermute | solution.py:54
  10.9 8.6 %collective-permute-start = (bf16[64,1024]{1,0:T(8,128)(2,1)S(1)}, bf16[64,1024]{1,0:T(8,128)(2,1)S(1)}, u32[]{:S(2)}, u32[]{:S(2)}) collective-permute-start(bf16[64,1024]{1,0:T(8,128)(2,1)S(1)} %attend.1), channel_id=1, source_target_pairs={{4,0},{8,4},{12,8},{0,12},{5,1},{9,5},{13,9},{1,13},{6,2},{10,6},{... | collective-permute-start | bytes 393224 | tf_op jit(solution)/shard_map/ppermute | solution.py:54
  22.5 12.4 %collective-permute-start.3 = (bf16[4,16,1024]{2,1,0:T(8,128)(2,1)S(1)}, bf16[4,16,1024]{2,1,0:T(8,128)(2,1)S(1)}, u32[]{:S(2)}, u32[]{:S(2)}) collective-permute-start(bf16[4,16,1024]{2,1,0:T(8,128)(2,1)S(1)} %get-tuple-element.36), channel_id=1, source_target_pairs={{0,1},{1,0},{2,3},{3,2},{4,5},{5,4},{6,7},{7,6},{8,9},{9,8},{10,11... | collective-permute-start | bytes 393224 | tf_op jit(solution)/shard_map/ppermute | solution.py:74
  23.3 7.1 %collective-permute-start.8 = (f32[16,64]{1,0:T(8,128)S(1)}, f32[16,64]{1,0:T(8,128)S(1)}, u32[]{:S(2)}, u32[]{:S(2)}) collective-permute-start(f32[16,64]{1,0:T(8,128)S(1)} %pad_maximum_fusion.1), channel_id=1, source_target_pairs={{12,0},{0,4},{4,8},{8,12},{13,1},{1,5},{5,9},{9,13},{14,2},{2,6},{... | collective-permute-start | bytes 12296 | tf_op jit(solution)/shard_map/ppermute | solution.py:54
  26.6 5.6 %collective-permute-start.7 = (f32[16,64]{1,0:T(8,128)S(1)}, f32[16,64]{1,0:T(8,128)S(1)}, u32[]{:S(2)}, u32[]{:S(2)}) collective-permute-start(f32[16,64]{1,0:T(8,128)S(1)} %pad_maximum_fusion.1), channel_id=1, source_target_pairs={{8,0},{12,4},{0,8},{4,12},{9,1},{13,5},{1,9},{5,13},{10,2},{14,6},... | collective-permute-start | bytes 12296 | tf_op jit(solution)/shard_map/ppermute | solution.py:54
  28.2 4.0 %collective-permute-start.6 = (f32[16,64]{1,0:T(8,128)S(1)}, f32[16,64]{1,0:T(8,128)S(1)}, u32[]{:S(2)}, u32[]{:S(2)}) collective-permute-start(f32[16,64]{1,0:T(8,128)S(1)} %pad_maximum_fusion.1), channel_id=1, source_target_pairs={{4,0},{8,4},{12,8},{0,12},{5,1},{9,5},{13,9},{1,13},{6,2},{10,6},{... | collective-permute-start | bytes 12296 | tf_op jit(solution)/shard_map/ppermute | solution.py:54
  28.9 7.0 %collective-permute-start.4 = (bf16[4,16,1024]{2,1,0:T(8,128)(2,1)S(1)}, bf16[4,16,1024]{2,1,0:T(8,128)(2,1)S(1)}, u32[]{:S(2)}, u32[]{:S(2)}) collective-permute-start(bf16[4,16,1024]{2,1,0:T(8,128)(2,1)S(1)} %get-tuple-element.37), channel_id=1, source_target_pairs={{0,2},{1,3},{2,0},{3,1},{4,6},{5,7},{6,4},{7,5},{8,10},{9,11},{10,... | collective-permute-start | bytes 393224 | tf_op jit(solution)/shard_map/ppermute | solution.py:74
  30.4 5.8 %collective-permute-start.5 = (bf16[4,16,1024]{2,1,0:T(8,128)(2,1)S(1)}, bf16[4,16,1024]{2,1,0:T(8,128)(2,1)S(1)}, u32[]{:S(2)}, u32[]{:S(2)}) collective-permute-start(bf16[4,16,1024]{2,1,0:T(8,128)(2,1)S(1)} %get-tuple-element.38), channel_id=1, source_target_pairs={{0,3},{1,2},{2,1},{3,0},{4,7},{5,6},{6,5},{7,4},{8,11},{9,10},{10,... | collective-permute-start | bytes 393224 | tf_op jit(solution)/shard_map/ppermute | solution.py:74
  32.2 4.1 %collective-permute-start.9 = (bf16[16,1024]{1,0:T(8,128)(2,1)S(1)}, bf16[16,1024]{1,0:T(8,128)(2,1)S(1)}, u32[]{:S(2)}, u32[]{:S(2)}) collective-permute-start(bf16[16,1024]{1,0:T(8,128)(2,1)S(1)} %get-tuple-element.50), channel_id=1, source_target_pairs={{4,0},{8,4},{12,8},{0,12},{5,1},{9,5},{13,9},{1,13},{6,2},{10,6},{... | collective-permute-start | bytes 98312 | tf_op jit(solution)/shard_map/ppermute | solution.py:68
  34.4 4.8 %collective-permute-start.10 = (bf16[16,1024]{1,0:T(8,128)(2,1)S(1)}, bf16[16,1024]{1,0:T(8,128)(2,1)S(1)}, u32[]{:S(2)}, u32[]{:S(2)}) collective-permute-start(bf16[16,1024]{1,0:T(8,128)(2,1)S(1)} %get-tuple-element.51), channel_id=1, source_target_pairs={{8,0},{12,4},{0,8},{4,12},{9,1},{13,5},{1,9},{5,13},{10,2},{14,6},... | collective-permute-start | bytes 98312 | tf_op jit(solution)/shard_map/ppermute | solution.py:68
  34.9 5.7 %collective-permute-start.11 = (bf16[16,1024]{1,0:T(8,128)(2,1)S(1)}, bf16[16,1024]{1,0:T(8,128)(2,1)S(1)}, u32[]{:S(2)}, u32[]{:S(2)}) collective-permute-start(bf16[16,1024]{1,0:T(8,128)(2,1)S(1)} %get-tuple-element.52), channel_id=1, source_target_pairs={{12,0},{0,4},{4,8},{8,12},{13,1},{1,5},{5,9},{9,13},{14,2},{2,6},{... | collective-permute-start | bytes 98312 | tf_op jit(solution)/shard_map/ppermute | solution.py:68
  41.3 8.3 %collective-permute-start.14 = (bf16[64,1024]{1,0:T(8,128)(2,1)S(1)}, bf16[64,1024]{1,0:T(8,128)(2,1)S(1)}, u32[]{:S(2)}, u32[]{:S(2)}) collective-permute-start(bf16[64,1024]{1,0:T(8,128)(2,1)S(1)} %bitcast.41), channel_id=1, source_target_pairs={{12,0},{0,4},{4,8},{8,12},{13,1},{1,5},{5,9},{9,13},{14,2},{2,6},{... | collective-permute-start | bytes 393224 | tf_op jit(solution)/shard_map/ppermute | solution.py:54
  41.3 11.9 %collective-permute-start.13 = (bf16[64,1024]{1,0:T(8,128)(2,1)S(1)}, bf16[64,1024]{1,0:T(8,128)(2,1)S(1)}, u32[]{:S(2)}, u32[]{:S(2)}) collective-permute-start(bf16[64,1024]{1,0:T(8,128)(2,1)S(1)} %bitcast.42), channel_id=1, source_target_pairs={{8,0},{12,4},{0,8},{4,12},{9,1},{13,5},{1,9},{5,13},{10,2},{14,6},... | collective-permute-start | bytes 393224 | tf_op jit(solution)/shard_map/ppermute | solution.py:54
  42.1 11.1 %collective-permute-start.12 = (bf16[64,1024]{1,0:T(8,128)(2,1)S(1)}, bf16[64,1024]{1,0:T(8,128)(2,1)S(1)}, u32[]{:S(2)}, u32[]{:S(2)}) collective-permute-start(bf16[64,1024]{1,0:T(8,128)(2,1)S(1)} %bitcast.43), channel_id=1, source_target_pairs={{4,0},{8,4},{12,8},{0,12},{5,1},{9,5},{13,9},{1,13},{6,2},{10,6},{... | collective-permute-start | bytes 393224 | tf_op jit(solution)/shard_map/ppermute | solution.py:54
  45.1 9.5 %collective-permute-start.16 = (bf16[1,64,1024]{2,1,0:T(8,128)(2,1)S(1)}, bf16[1,64,1024]{2,1,0:T(8,128)(2,1)S(1)}, u32[]{:S(2)}, u32[]{:S(2)}) collective-permute-start(bf16[1,64,1024]{2,1,0:T(8,128)(2,1)S(1)} %bitcast.44), channel_id=1, source_target_pairs={{0,2},{1,3},{2,0},{3,1},{4,6},{5,7},{6,4},{7,5},{8,10},{9,11},{10,... | collective-permute-start | bytes 393224 | tf_op jit(solution)/shard_map/ppermute | solution.py:74
  46.3 8.5 %collective-permute-start.15 = (bf16[1,64,1024]{2,1,0:T(8,128)(2,1)S(1)}, bf16[1,64,1024]{2,1,0:T(8,128)(2,1)S(1)}, u32[]{:S(2)}, u32[]{:S(2)}) collective-permute-start(bf16[1,64,1024]{2,1,0:T(8,128)(2,1)S(1)} %bitcast.45), channel_id=1, source_target_pairs={{0,1},{1,0},{2,3},{3,2},{4,5},{5,4},{6,7},{7,6},{8,9},{9,8},{10,11... | collective-permute-start | bytes 393224 | tf_op jit(solution)/shard_map/ppermute | solution.py:74
  49.5 5.9 %collective-permute-start.25 = (bf16[1,64,1024]{2,1,0:T(8,128)(2,1)S(1)}, bf16[1,64,1024]{2,1,0:T(8,128)(2,1)S(1)}, u32[]{:S(2)}, u32[]{:S(2)}) collective-permute-start(bf16[1,64,1024]{2,1,0:T(8,128)(2,1)S(1)} %bitcast.49), channel_id=1, source_target_pairs={{0,2},{1,3},{2,0},{3,1},{4,6},{5,7},{6,4},{7,5},{8,10},{9,11},{10,... | collective-permute-start | bytes 393224 | tf_op jit(solution)/shard_map/ppermute | solution.py:74
  53.2 2.3 %collective-permute-start.24 = (bf16[1,64,1024]{2,1,0:T(8,128)(2,1)S(1)}, bf16[1,64,1024]{2,1,0:T(8,128)(2,1)S(1)}, u32[]{:S(2)}, u32[]{:S(2)}) collective-permute-start(bf16[1,64,1024]{2,1,0:T(8,128)(2,1)S(1)} %bitcast.50), channel_id=1, source_target_pairs={{0,1},{1,0},{2,3},{3,2},{4,5},{5,4},{6,7},{7,6},{8,9},{9,8},{10,11... | collective-permute-start | bytes 393224 | tf_op jit(solution)/shard_map/ppermute | solution.py:74
  53.2 6.4 %collective-permute-start.22 = (bf16[1,64,1024]{2,1,0:T(8,128)(2,1)S(1)}, bf16[1,64,1024]{2,1,0:T(8,128)(2,1)S(1)}, u32[]{:S(2)}, u32[]{:S(2)}) collective-permute-start(bf16[1,64,1024]{2,1,0:T(8,128)(2,1)S(1)} %bitcast.54), channel_id=1, source_target_pairs={{0,2},{1,3},{2,0},{3,1},{4,6},{5,7},{6,4},{7,5},{8,10},{9,11},{10,... | collective-permute-start | bytes 393224 | tf_op jit(solution)/shard_map/ppermute | solution.py:74
  54.6 5.0 %collective-permute-start.21 = (bf16[1,64,1024]{2,1,0:T(8,128)(2,1)S(1)}, bf16[1,64,1024]{2,1,0:T(8,128)(2,1)S(1)}, u32[]{:S(2)}, u32[]{:S(2)}) collective-permute-start(bf16[1,64,1024]{2,1,0:T(8,128)(2,1)S(1)} %bitcast.55), channel_id=1, source_target_pairs={{0,1},{1,0},{2,3},{3,2},{4,5},{5,4},{6,7},{7,6},{8,9},{9,8},{10,11... | collective-permute-start | bytes 393224 | tf_op jit(solution)/shard_map/ppermute | solution.py:74
  54.9 7.1 %collective-permute-start.19 = (bf16[1,64,1024]{2,1,0:T(8,128)(2,1)S(1)}, bf16[1,64,1024]{2,1,0:T(8,128)(2,1)S(1)}, u32[]{:S(2)}, u32[]{:S(2)}) collective-permute-start(bf16[1,64,1024]{2,1,0:T(8,128)(2,1)S(1)} %bitcast.59), channel_id=1, source_target_pairs={{0,2},{1,3},{2,0},{3,1},{4,6},{5,7},{6,4},{7,5},{8,10},{9,11},{10,... | collective-permute-start | bytes 393224 | tf_op jit(solution)/shard_map/ppermute | solution.py:74
  55.5 6.5 %collective-permute-start.18 = (bf16[1,64,1024]{2,1,0:T(8,128)(2,1)S(1)}, bf16[1,64,1024]{2,1,0:T(8,128)(2,1)S(1)}, u32[]{:S(2)}, u32[]{:S(2)}) collective-permute-start(bf16[1,64,1024]{2,1,0:T(8,128)(2,1)S(1)} %bitcast.60), channel_id=1, source_target_pairs={{0,1},{1,0},{2,3},{3,2},{4,5},{5,4},{6,7},{7,6},{8,9},{9,8},{10,11... | collective-permute-start | bytes 393224 | tf_op jit(solution)/shard_map/ppermute | solution.py:74
  55.5 6.5 %collective-permute-start.17 = (bf16[1,64,1024]{2,1,0:T(8,128)(2,1)S(1)}, bf16[1,64,1024]{2,1,0:T(8,128)(2,1)S(1)}, u32[]{:S(2)}, u32[]{:S(2)}) collective-permute-start(bf16[1,64,1024]{2,1,0:T(8,128)(2,1)S(1)} %collective-permute-done.16.refs_2_), channel_id=1, source_target_pairs={{0,1},{1,0},{2,3},{3,2},{4,5},{5,4},{6,7},{7,6},{8,9},{9,8},{10,11... | collective-permute-start | bytes 393224 | tf_op jit(solution)/shard_map/ppermute | solution.py:74
  59.6 2.4 %collective-permute-start.26 = (bf16[1,64,1024]{2,1,0:T(8,128)(2,1)S(1)}, bf16[1,64,1024]{2,1,0:T(8,128)(2,1)S(1)}, u32[]{:S(2)}, u32[]{:S(2)}) collective-permute-start(bf16[1,64,1024]{2,1,0:T(8,128)(2,1)S(1)} %collective-permute-done.25.refs_14_), channel_id=1, source_target_pairs={{0,1},{1,0},{2,3},{3,2},{4,5},{5,4},{6,7},{7,6},{8,9},{9,8},{10,11... | collective-permute-start | bytes 393224 | tf_op jit(solution)/shard_map/ppermute | solution.py:74
  59.6 2.4 %collective-permute-start.23 = (bf16[1,64,1024]{2,1,0:T(8,128)(2,1)S(1)}, bf16[1,64,1024]{2,1,0:T(8,128)(2,1)S(1)}, u32[]{:S(2)}, u32[]{:S(2)}) collective-permute-start(bf16[1,64,1024]{2,1,0:T(8,128)(2,1)S(1)} %collective-permute-done.22.refs_10_), channel_id=1, source_target_pairs={{0,1},{1,0},{2,3},{3,2},{4,5},{5,4},{6,7},{7,6},{8,9},{9,8},{10,11... | collective-permute-start | bytes 393224 | tf_op jit(solution)/shard_map/ppermute | solution.py:74
  74.5 11.1 %collective-permute-start.27 = (bf16[4,128,256]{2,1,0:T(8,128)(2,1)S(1)}, bf16[4,128,256]{2,1,0:T(8,128)(2,1)S(1)}, u32[]{:S(2)}, u32[]{:S(2)}) collective-permute-start(bf16[4,128,256]{2,1,0:T(8,128)(2,1)S(1)} %get-tuple-element.60.refs_0_), channel_id=1, source_target_pairs={{0,2},{1,3},{2,0},{3,1},{4,6},{5,7},{6,4},{7,5},{8,10},{9,11},{10,... | collective-permute-start | bytes 786440 | tf_op jit(solution)/shard_map/ppermute | solution.py:74
  76.0 10.8 %collective-permute-start.30 = (bf16[4,128,256]{2,1,0:T(8,128)(2,1)S(1)}, bf16[4,128,256]{2,1,0:T(8,128)(2,1)S(1)}, u32[]{:S(2)}, u32[]{:S(2)}) collective-permute-start(bf16[4,128,256]{2,1,0:T(8,128)(2,1)S(1)} %get-tuple-element.60.refs_0_), channel_id=1, source_target_pairs={{0,1},{1,0},{2,3},{3,2},{4,5},{5,4},{6,7},{7,6},{8,9},{9,8},{10,11... | collective-permute-start | bytes 786440 | tf_op jit(solution)/shard_map/ppermute | solution.py:74
  85.6 1.7 %collective-permute-start.31 = (bf16[4,128,256]{2,1,0:T(8,128)(2,1)S(1)}, bf16[4,128,256]{2,1,0:T(8,128)(2,1)S(1)}, u32[]{:S(2)}, u32[]{:S(2)}) collective-permute-start(bf16[4,128,256]{2,1,0:T(8,128)(2,1)S(1)} %collective-permute-done.27.refs_2_), channel_id=1, source_target_pairs={{0,1},{1,0},{2,3},{3,2},{4,5},{5,4},{6,7},{7,6},{8,9},{9,8},{10,11... | collective-permute-start | bytes 786440 | tf_op jit(solution)/shard_map/ppermute | solution.py:74
  86.2 8.3 %collective-permute-start.29 = (bf16[4,128,256]{2,1,0:T(8,128)(2,1)S(1)}, bf16[4,128,256]{2,1,0:T(8,128)(2,1)S(1)}, u32[]{:S(2)}, u32[]{:S(2)}) collective-permute-start(bf16[4,128,256]{2,1,0:T(8,128)(2,1)S(1)} %hidden.3.refs_0_), channel_id=1, source_target_pairs={{0,2},{1,3},{2,0},{3,1},{4,6},{5,7},{6,4},{7,5},{8,10},{9,11},{10,... | collective-permute-start | bytes 786440 | tf_op jit(solution)/shard_map/ppermute | solution.py:74
  86.8 7.7 %collective-permute-start.28 = (bf16[4,128,256]{2,1,0:T(8,128)(2,1)S(1)}, bf16[4,128,256]{2,1,0:T(8,128)(2,1)S(1)}, u32[]{:S(2)}, u32[]{:S(2)}) collective-permute-start(bf16[4,128,256]{2,1,0:T(8,128)(2,1)S(1)} %hidden.3.refs_0_), channel_id=1, source_target_pairs={{0,1},{1,0},{2,3},{3,2},{4,5},{5,4},{6,7},{7,6},{8,9},{9,8},{10,11... | collective-permute-start | bytes 786440 | tf_op jit(solution)/shard_map/ppermute | solution.py:74
  102.0 18.7 %all-to-all-start = ((bf16[16,16,1024]{2,1,0:T(8,128)(2,1)}), bf16[16,16,1024]{2,1,0:T(8,128)(2,1)S(1)}, u32[]{:S(2)}, u32[]{:S(2)}) async-start(bf16[16,16,1024]{2,1,0:T(8,128)(2,1)} %bitcast.27), calls=%async_computation | async-start | bytes 1048576 | tf_op jit(solution)/shard_map/all_to_all | solution.py:479
  (10 other events, 36.2 us)

commit v2 on v1

--- a/solution.py
+++ b/solution.py
@@ -103,9 +103,7 @@
 
 
 def attend(q, k, v, seg):
-    out_shape = jax.ShapeDtypeStruct(q.shape, BF16)
-    grant = room(q, k, v, out_shape)
-    return pl.pallas_call(attend_kernel, out_shape=out_shape, compiler_params=grant, name="attend")(q, k, v, seg)
+    return pl.pallas_call(attend_kernel, out_shape=jax.ShapeDtypeStruct(q.shape, BF16), name="attend")(q, k, v, seg)
 
 
 def project_kernel(place_ref, *refs, pieces, n_count):
@@ -172,14 +170,14 @@
     )(place, gain_here, *shares, *resid)
 
 
-def base_kernel(place_ref, gain_ref, target_ref, *refs):
+def base_kernel(place_ref, inverse_ref, target_ref, *refs):
     pieces, base_ref = refs[:-1], refs[-1]
     width = pieces[0].shape[2]
     part = target_ref.shape[0]
     for i, piece in enumerate(pieces):
         col = pl.multiple_of(place_ref[1 + i] * width, 128)
         own = piece[0, pl.ds(pl.multiple_of(place_ref[0] * part, 8), part), :].astype(F32)
-        base_ref[:, pl.ds(col, width)] = own / gain_ref[:, pl.ds(col, width)] - target_ref[:, pl.ds(col, width)].astype(F32)
+        base_ref[:, pl.ds(col, width)] = own * inverse_ref[:, pl.ds(col, width)] - target_ref[:, pl.ds(col, width)].astype(F32)
 
 
 def base_of(place, gain, target, pieces):
@@ -228,8 +226,7 @@
                 here = pl.ds(pl.multiple_of(c * some, 16), some)
                 sums = 0.0
                 for first in range(0, model_width, wide):
-                    inverse = 1.0 / norm_ref[:, first : first + wide]
-                    stream = rows_ref[here, first : first + wide].astype(F32) * inverse
+                    stream = rows_ref[here, first : first + wide].astype(F32) * norm_ref[:, first : first + wide]
                     sums += jnp.sum(stream * stream, axis=1, keepdims=True)
                 scale_ref[here, :] = jnp.broadcast_to(lax.rsqrt(sums / model_width + 1e-06), (some, 128))
 
@@ -438,22 +435,25 @@
     n_place = jnp.concatenate([n_here[None].astype(jnp.int32), w_index])
     w_place = jnp.concatenate([w_here[None].astype(jnp.int32), w_index])
 
+    own_resid = lax.dynamic_slice_in_dim(residual, n_here * part, part, 0)
+    resid_pieces = wide_exchange(lambda w: lax.dynamic_slice_in_dim(own_resid, w * out_width, out_width, 1), attended)
+    gain_here = lax.dynamic_slice_in_dim(norm_gain, w_here * out_width, out_width, 0)[None]
+    inverse = 1.0 / norm_gain[None]
     packed = jnp.concatenate([expert_ids.astype(F32).T, gate_weights.T], axis=0)
-    packed, _ = lax.optimization_barrier((packed, attended))
+    packed, gain_here, inverse, att_pieces = lax.optimization_barrier((packed, gain_here, inverse, att_pieces))
+
+    shares = project(n_place, att_pieces, o_weight, n_count)
+    shares = [shares[0]] + [narrow_flip(shares[j], j) for j in range(1, n_count)]
+    scaled = stream_of(n_place, gain_here, shares, resid_pieces).reshape(w_count * part, out_width)
+
+    wide_rows, _ = wide_pieces(scaled)
+    pieces = []
+    for rows in wide_rows:
+        pieces.append(narrow_pieces(rows)[0])
+    packed, _ = lax.optimization_barrier((packed, scaled))
     packed_pieces, _ = wide_pieces(packed)
-    shares = project(n_place, att_pieces, o_weight, n_count)
-    packed_pieces, _ = lax.optimization_barrier((packed_pieces, shares[0]))
     each_wide = [piece[i] for piece in packed_pieces for i in range(piece.shape[0])]
     slot, gate = routing(w_place, jnp.concatenate(each_wide, axis=1), experts)
-    gain_here = lax.dynamic_slice_in_dim(norm_gain, w_here * out_width, out_width, 0)[None]
-    own_resid = lax.dynamic_slice_in_dim(residual, n_here * part, part, 0)
-    resid_pieces = wide_exchange(lambda w: lax.dynamic_slice_in_dim(own_resid, w * out_width, out_width, 1), shares[0])
-    shares = [shares[0]] + [narrow_flip(shares[j], j) for j in range(1, n_count)]
-    shares, slot, gate = lax.optimization_barrier((shares, slot, gate))
-    scaled = stream_of(n_place, gain_here, shares, resid_pieces).reshape(w_count * part, out_width)
-
-    wide_rows, _ = wide_pieces(scaled)
-    pieces = [narrow_pieces(rows)[0] for rows in wide_rows]
     if len(pieces) == 1 and w_count > 1:
         rows = jnp.stack(pieces[0])[n_here ^ jnp.arange(n_count)].reshape(n_count, w_count, w_count, part, -1)
         pieces = [[rows.transpose(2, 0, 3, 1, 4).reshape(1, -1, model_width)]]
@@ -461,12 +461,12 @@
     else:
         own_place = w_place
     some = experts // PARTS if experts % (2 * PARTS) == 0 else experts
-    norm, rows_of = norm_gain[None], []
+    norm, rows_of = inverse, []
     for first in range(0, experts, some):
         mine, norm = hidden_of(n_place, slot, norm, pieces, w_gate, w_up, slots, first, some)
         rows_of.append(mine)
     own_pieces, _ = lax.optimization_barrier(([group[0] for group in pieces], rows_of[-1]))
-    base = base_of(own_place, norm_gain[None], target, own_pieces)
+    base = base_of(own_place, inverse, target, own_pieces)
     partial_sum = None
     for i in range(len(rows_of)):
         later = i + 1 < len(rows_of)

time: 122 us -> 121 us (level)
  waiting for transfers between devices: 41.4 us -> 37.5 us
  starting transfers between devices: 33.7 us -> 37.5 us
  local copies, waits for them, and re-layouts: 7.4 us -> 4.21 us
  Pallas kernels: 36.5 us -> 38.1 us
    ppermute x9, waiting for transfers between devices: 12.4 us -> 7.69 us  [wide_pieces(): lax.ppermute(rows, 'wide', [((i + step) % count, i) for i in range(count)])]
    unnamed x16 -> x6, local copies, waits for them, and re-layouts: 5.69 us -> 2.5 us
    ppermute x3, starting transfers between devices: 3.02 us -> 6.03 us  [wide_exchange(): found.append(lax.ppermute(blocks[step - 1], 'wide', pairs)[None])]
    ppermute x3, waiting for transfers between devices: 4.4 us -> 6.16 us  [wide_exchange(): found.append(lax.ppermute(blocks[step - 1], 'wide', pairs)[None])]
    pallas_call x1, Pallas kernels: 1.88 us -> 3.56 us  [attend(): pl.pallas_call(attend_kernel, out_shape=jax.ShapeDtypeStruct(q.shape, BF1...]
  transfers between devices with their start and end apart: 34 -> 34, of which waited for: 14 -> 13; matrix products, arithmetic and copies ran while one was open for 3% -> 3% of each run, Pallas kernels for 13% -> 13%
where the time goes in v2:
time: 121 us; the launch traced here: 120 us
  Pallas kernels  38.1 us (31%)
  starting transfers between devices  37.5 us (31%)
  waiting for transfers between devices  37.5 us (31%)
  local copies, waits for them, and re-layouts  4.21 us (3%)
  other arithmetic  3.02 us (2%)
    pallas_call x2, Pallas kernels, hidden_of(): pl.pallas_call(functools.partial(hidden_kernel, groups=[len(g) for g in p...  20.1 us
    ppermute x9, starting transfers between devices, wide_pieces(): lax.ppermute(rows, 'wide', [((i + step) % count, i) for i in range(count)])  15.8 us
    all_to_all x1, waiting for transfers between devices, body(): lax.all_to_all(partial_sum.reshape(w_count * n_count, part, -1), ('wide',...  13.7 us
    pallas_call x2, Pallas kernels, combine(): pl.pallas_call(functools.partial(combine_kernel, n_count=n_count, w_count...  11.2 us
    ppermute x21, starting transfers between devices, narrow_flip(): return lax.ppermute(rows, 'narrow', [(i, i ^ bit) for i in range(count)])  10.8 us
    ppermute x21, waiting for transfers between devices, narrow_flip(): return lax.ppermute(rows, 'narrow', [(i, i ^ bit) for i in range(count)])  9.96 us
    ppermute x9, waiting for transfers between devices, wide_pieces(): lax.ppermute(rows, 'wide', [((i + step) % count, i) for i in range(count)])  7.69 us
    ppermute x3, waiting for transfers between devices, wide_exchange(): found.append(lax.ppermute(blocks[step - 1], 'wide', pairs)[None])  6.16 us
  transfers between devices with their start and end apart: 34, of which 13 were waited for; matrix products, arithmetic and copies ran while one was open for 3% of the time, Pallas kernels for 13%

profile of v2, /device:TPU:0, one launch (start us, length us, event | category | flops | bytes accessed | tf_op | source)
XLA Modules:
  0.0 120.5 jit_solution(11139833712044240902)
XLA Ops:
  0.0 3.6 %attend.1 = bf16[64,1024]{1,0:T(8,128)(2,1)} custom-call(bf16[64,1024]{1,0:T(8,128)(2,1)} %q_ref.1, bf16[64,1024]{1,0:T(8,128)(2,1)} %k_ref.1, bf16[64,1024]{1,0:T(8,128)(2,1)} %v_ref.1, s32[1,64]{1,0:T(1,128)} %seg_ref.1), custom_call_target="tpu_custom_call" | custom-call | tf_op jit(solution)/shard_map/attend/pallas_call | solution.py:106
  3.6 3.1 %collective-permute-start.2 = (bf16[64,1024]{1,0:T(8,128)(2,1)}, bf16[64,1024]{1,0:T(8,128)(2,1)S(1)}, u32[]{:S(2)}, u32[]{:S(2)}) collective-permute-start(bf16[64,1024]{1,0:T(8,128)(2,1)} %attend.1), channel_id=1, source_target_pairs={{12,0},{0,4},{4,8},{8,12},{13,1},{1,5},{5,9},{9,13},{14,2},{2,6},{... | collective-permute-start | bytes 393224 | tf_op jit(solution)/shard_map/ppermute | solution.py:54
  6.6 2.6 %collective-permute-start.1 = (bf16[64,1024]{1,0:T(8,128)(2,1)}, bf16[64,1024]{1,0:T(8,128)(2,1)S(1)}, u32[]{:S(2)}, u32[]{:S(2)}) collective-permute-start(bf16[64,1024]{1,0:T(8,128)(2,1)} %attend.1), channel_id=1, source_target_pairs={{8,0},{12,4},{0,8},{4,12},{9,1},{13,5},{1,9},{5,13},{10,2},{14,6},... | collective-permute-start | bytes 393224 | tf_op jit(solution)/shard_map/ppermute | solution.py:54
  9.2 1.3 %collective-permute-start = (bf16[64,1024]{1,0:T(8,128)(2,1)}, bf16[64,1024]{1,0:T(8,128)(2,1)S(1)}, u32[]{:S(2)}, u32[]{:S(2)}) collective-permute-start(bf16[64,1024]{1,0:T(8,128)(2,1)} %attend.1), channel_id=1, source_target_pairs={{4,0},{8,4},{12,8},{0,12},{5,1},{9,5},{13,9},{1,13},{6,2},{10,6},{... | collective-permute-start | bytes 393224 | tf_op jit(solution)/shard_map/ppermute | solution.py:54
  13.4 4.6 %collective-permute-done.1 = bf16[64,1024]{1,0:T(8,128)(2,1)S(1)} collective-permute-done((bf16[64,1024]{1,0:T(8,128)(2,1)}, bf16[64,1024]{1,0:T(8,128)(2,1)S(1)}, u32[]{:S(2)}, u32[]{:S(2)}) %collective-permute-start.1) | collective-permute-done | bytes 131104 | tf_op jit(solution)/shard_map/ppermute | solution.py:54
  18.1 1.6 %copy-done = bf16[1024,1024]{1,0:T(8,128)(2,1)S(1)} copy-done((bf16[1024,1024]{1,0:T(8,128)(2,1)S(1)}, bf16[1024,1024]{1,0:T(8,128)(2,1)}, u32[]{:S(2)}) %copy-start) | copy-done | bytes 2097176
  20.6 1.3 %project.1 = (f32[4,16,1024]{2,1,0:T(8,128)S(1)}, bf16[4,16,1024]{2,1,0:T(8,128)(2,1)S(1)}, bf16[4,16,1024]{2,1,0:T(8,128)(2,1)S(1)}, bf16[4,16,1024]{2,1,0:T(8,128)(2,1)S(1)}) custom-call(s32[5]{0:T(128)S(1)} %get-tuple-element.63.place_ref, bf16[1,64,1024]{2,1,0:T(8,128)(2,1)S(1)} %bitcast.57, bf16[1,64,1024]{2,1,0:T(8,128)(2,1)S(1)} %bitcast.62, ...), custom_call_target="tpu_custom_call" | custom-call | tf_op jit(solution)/shard_map/project/pallas_call | solution.py:129
  22.0 1.6 %collective-permute-start.4 = (bf16[4,16,1024]{2,1,0:T(8,128)(2,1)S(1)}, bf16[4,16,1024]{2,1,0:T(8,128)(2,1)S(1)}, u32[]{:S(2)}, u32[]{:S(2)}) collective-permute-start(bf16[4,16,1024]{2,1,0:T(8,128)(2,1)S(1)} %get-tuple-element.40), channel_id=1, source_target_pairs={{0,2},{1,3},{2,0},{3,1},{4,6},{5,7},{6,4},{7,5},{8,10},{9,11},{10,... | collective-permute-start | bytes 393224 | tf_op jit(solution)/shard_map/ppermute | solution.py:74
  24.8 4.4 %collective-permute-start.6 = (bf16[16,1024]{1,0:T(8,128)(2,1)S(1)}, bf16[16,1024]{1,0:T(8,128)(2,1)S(1)}, u32[]{:S(2)}, u32[]{:S(2)}) collective-permute-start(bf16[16,1024]{1,0:T(8,128)(2,1)S(1)} %get-tuple-element.42), channel_id=1, source_target_pairs={{4,0},{8,4},{12,8},{0,12},{5,1},{9,5},{13,9},{1,13},{6,2},{10,6},{... | collective-permute-start | bytes 98312 | tf_op jit(solution)/shard_map/ppermute | solution.py:68
  30.8 1.2 %collective-permute-start.8 = (bf16[16,1024]{1,0:T(8,128)(2,1)S(1)}, bf16[16,1024]{1,0:T(8,128)(2,1)S(1)}, u32[]{:S(2)}, u32[]{:S(2)}) collective-permute-start(bf16[16,1024]{1,0:T(8,128)(2,1)S(1)} %get-tuple-element.44), channel_id=1, source_target_pairs={{12,0},{0,4},{4,8},{8,12},{13,1},{1,5},{5,9},{9,13},{14,2},{2,6},{... | collective-permute-start | bytes 98312 | tf_op jit(solution)/shard_map/ppermute | solution.py:68
  32.1 2.0 %collective-permute-done.7 = bf16[16,1024]{1,0:T(8,128)(2,1)S(1)} collective-permute-done((bf16[16,1024]{1,0:T(8,128)(2,1)S(1)}, bf16[16,1024]{1,0:T(8,128)(2,1)S(1)}, u32[]{:S(2)}, u32[]{:S(2)}) %collective-permute-start.7) | collective-permute-done | bytes 32800 | tf_op jit(solution)/shard_map/ppermute | solution.py:68
  34.0 3.0 %collective-permute-done.8 = bf16[16,1024]{1,0:T(8,128)(2,1)S(1)} collective-permute-done((bf16[16,1024]{1,0:T(8,128)(2,1)S(1)}, bf16[16,1024]{1,0:T(8,128)(2,1)S(1)}, u32[]{:S(2)}, u32[]{:S(2)}) %collective-permute-start.8) | collective-permute-done | bytes 32800 | tf_op jit(solution)/shard_map/ppermute | solution.py:68
  37.7 2.6 %collective-permute-start.13 = (f32[16,64]{1,0:T(8,128)S(1)}, f32[16,64]{1,0:T(8,128)S(1)}, u32[]{:S(2)}, u32[]{:S(2)}) collective-permute-start(f32[16,64]{1,0:T(8,128)S(1)} %pad_maximum_fusion.1), channel_id=1, source_target_pairs={{8,0},{12,4},{0,8},{4,12},{9,1},{13,5},{1,9},{5,13},{10,2},{14,6},... | collective-permute-start | bytes 12296 | tf_op jit(solution)/shard_map/ppermute | solution.py:54
  40.3 1.2 %collective-permute-start.12 = (f32[16,64]{1,0:T(8,128)S(1)}, f32[16,64]{1,0:T(8,128)S(1)}, u32[]{:S(2)}, u32[]{:S(2)}) collective-permute-start(f32[16,64]{1,0:T(8,128)S(1)} %pad_maximum_fusion.1), channel_id=1, source_target_pairs={{4,0},{8,4},{12,8},{0,12},{5,1},{9,5},{13,9},{1,13},{6,2},{10,6},{... | collective-permute-start | bytes 12296 | tf_op jit(solution)/shard_map/ppermute | solution.py:54
  42.3 1.2 %collective-permute-start.10 = (bf16[64,1024]{1,0:T(8,128)(2,1)S(1)}, bf16[64,1024]{1,0:T(8,128)(2,1)S(1)}, u32[]{:S(2)}, u32[]{:S(2)}) collective-permute-start(bf16[64,1024]{1,0:T(8,128)(2,1)S(1)} %bitcast.34), channel_id=1, source_target_pairs={{8,0},{12,4},{0,8},{4,12},{9,1},{13,5},{1,9},{5,13},{10,2},{14,6},... | collective-permute-start | bytes 393224 | tf_op jit(solution)/shard_map/ppermute | solution.py:54
  43.6 2.9 %collective-permute-start.9 = (bf16[64,1024]{1,0:T(8,128)(2,1)S(1)}, bf16[64,1024]{1,0:T(8,128)(2,1)S(1)}, u32[]{:S(2)}, u32[]{:S(2)}) collective-permute-start(bf16[64,1024]{1,0:T(8,128)(2,1)S(1)} %bitcast.35), channel_id=1, source_target_pairs={{4,0},{8,4},{12,8},{0,12},{5,1},{9,5},{13,9},{1,13},{6,2},{10,6},{... | collective-permute-start | bytes 393224 | tf_op jit(solution)/shard_map/ppermute | solution.py:54
  46.5 1.4 %collective-permute-start.16 = (bf16[1,64,1024]{2,1,0:T(8,128)(2,1)S(1)}, bf16[1,64,1024]{2,1,0:T(8,128)(2,1)S(1)}, u32[]{:S(2)}, u32[]{:S(2)}) collective-permute-start(bf16[1,64,1024]{2,1,0:T(8,128)(2,1)S(1)} %bitcast.36), channel_id=1, source_target_pairs={{0,2},{1,3},{2,0},{3,1},{4,6},{5,7},{6,4},{7,5},{8,10},{9,11},{10,... | collective-permute-start | bytes 393224 | tf_op jit(solution)/shard_map/ppermute | solution.py:74
  48.0 1.5 %collective-permute-done.11 = bf16[64,1024]{1,0:T(8,128)(2,1)S(1)} collective-permute-done((bf16[64,1024]{1,0:T(8,128)(2,1)S(1)}, bf16[64,1024]{1,0:T(8,128)(2,1)S(1)}, u32[]{:S(2)}, u32[]{:S(2)}) %collective-permute-start.11) | collective-permute-done | bytes 131104 | tf_op jit(solution)/shard_map/ppermute | solution.py:54
  49.4 1.4 %collective-permute-start.25 = (bf16[1,64,1024]{2,1,0:T(8,128)(2,1)S(1)}, bf16[1,64,1024]{2,1,0:T(8,128)(2,1)S(1)}, u32[]{:S(2)}, u32[]{:S(2)}) collective-permute-start(bf16[1,64,1024]{2,1,0:T(8,128)(2,1)S(1)} %bitcast.41), channel_id=1, source_target_pairs={{0,2},{1,3},{2,0},{3,1},{4,6},{5,7},{6,4},{7,5},{8,10},{9,11},{10,... | collective-permute-start | bytes 393224 | tf_op jit(solution)/shard_map/ppermute | solution.py:74
  50.9 1.6 %collective-permute-done.10 = bf16[64,1024]{1,0:T(8,128)(2,1)S(1)} collective-permute-done((bf16[64,1024]{1,0:T(8,128)(2,1)S(1)}, bf16[64,1024]{1,0:T(8,128)(2,1)S(1)}, u32[]{:S(2)}, u32[]{:S(2)}) %collective-permute-start.10) | collective-permute-done | bytes 131104 | tf_op jit(solution)/shard_map/ppermute | solution.py:54
  52.5 1.4 %collective-permute-start.22 = (bf16[1,64,1024]{2,1,0:T(8,128)(2,1)S(1)}, bf16[1,64,1024]{2,1,0:T(8,128)(2,1)S(1)}, u32[]{:S(2)}, u32[]{:S(2)}) collective-permute-start(bf16[1,64,1024]{2,1,0:T(8,128)(2,1)S(1)} %bitcast.46), channel_id=1, source_target_pairs={{0,2},{1,3},{2,0},{3,1},{4,6},{5,7},{6,4},{7,5},{8,10},{9,11},{10,... | collective-permute-start | bytes 393224 | tf_op jit(solution)/shard_map/ppermute | solution.py:74
  55.2 3.6 %collective-permute-done.22.refs_10_ = bf16[1,64,1024]{2,1,0:T(8,128)(2,1)S(1)} collective-permute-done((bf16[1,64,1024]{2,1,0:T(8,128)(2,1)S(1)}, bf16[1,64,1024]{2,1,0:T(8,128)(2,1)S(1)}, u32[]{:S(2)}, u32[]{:S(2)}) %collective-permute-start.22) | collective-permute-done | bytes 131104 | tf_op jit(solution)/shard_map/ppermute | solution.py:74
  59.3 1.8 %collective-permute-done.19.refs_6_ = bf16[1,64,1024]{2,1,0:T(8,128)(2,1)S(1)} collective-permute-done((bf16[1,64,1024]{2,1,0:T(8,128)(2,1)S(1)}, bf16[1,64,1024]{2,1,0:T(8,128)(2,1)S(1)}, u32[]{:S(2)}, u32[]{:S(2)}) %collective-permute-start.19) | collective-permute-done | bytes 131104 | tf_op jit(solution)/shard_map/ppermute | solution.py:74
  62.5 10.5 %hidden.2 = (bf16[4,128,256]{2,1,0:T(8,128)(2,1)S(1)}, f32[256,128]{1,0:T(8,128)S(1)}) custom-call(s32[5]{0:T(128)S(1)} %get-tuple-element.63.place_ref, s32[8,1,256]{2,1,0:T(1,128)S(1)} %get-tuple-element.47.slot_ref, f32[1,4096]{1,0:T(1,128)S(1)} %bitcast.58, bf16[1,64,1024]{2,1,0:T(8,128)(2,1)S(1)} %bitcast.38, ...), custom_call_target="tpu_custom_call" | custom-call | tf_op jit(solution)/shard_map/hidden/pallas_call | solution.py:269
  73.0 1.5 %collective-permute-start.27 = (bf16[4,128,256]{2,1,0:T(8,128)(2,1)S(1)}, bf16[4,128,256]{2,1,0:T(8,128)(2,1)S(1)}, u32[]{:S(2)}, u32[]{:S(2)}) collective-permute-start(bf16[4,128,256]{2,1,0:T(8,128)(2,1)S(1)} %get-tuple-element.54.refs_0_), channel_id=1, source_target_pairs={{0,2},{1,3},{2,0},{3,1},{4,6},{5,7},{6,4},{7,5},{8,10},{9,11},{10,... | collective-permute-start | bytes 786440 | tf_op jit(solution)/shard_map/ppermute | solution.py:74
  74.5 9.6 %hidden.3.refs_0_ = bf16[4,128,256]{2,1,0:T(8,128)(2,1)S(1)} custom-call(s32[5]{0:T(128)S(1)} %get-tuple-element.63.place_ref, s32[8,1,256]{2,1,0:T(1,128)S(1)} %get-tuple-element.47.slot_ref, f32[256,128]{1,0:T(8,128)S(1)} %get-tuple-element.48.norm_ref, bf16[1,64,1024]{2,1,0:T(8,128)(2,1)S(1)} %bitcast.39, ...), custom_call_target="tpu_custom_call" | custom-call | tf_op jit(solution)/shard_map/hidden/pallas_call | solution.py:269
  85.9 5.2 %combine.2.refs_8_ = f32[256,1024]{1,0:T(8,128)S(1)} custom-call(s32[5]{0:T(128)S(1)} %get-tuple-element.63.place_ref, s32[8,1,256]{2,1,0:T(1,128)S(1)} %get-tuple-element.47.slot_ref, f32[8,1,256]{2,1,0:T(1,128)S(1)} %get-tuple-element.53.gate_ref, bf16[4,128,256]{2,1,0:T(8,128)(2,1)S(1)} %get-tuple-element.54.refs_0_, ...), custom_call_target="tpu_custom_call" | custom-call | tf_op jit(solution)/shard_map/combine/pallas_call | solution.py:346
  91.1 1.9 %collective-permute-done.29.refs_2_ = bf16[4,128,256]{2,1,0:T(8,128)(2,1)S(1)} collective-permute-done((bf16[4,128,256]{2,1,0:T(8,128)(2,1)S(1)}, bf16[4,128,256]{2,1,0:T(8,128)(2,1)S(1)}, u32[]{:S(2)}, u32[]{:S(2)}) %collective-permute-start.29) | collective-permute-done | bytes 262176 | tf_op jit(solution)/shard_map/ppermute | solution.py:74
  93.0 1.5 %collective-permute-done.32.refs_3_ = bf16[4,128,256]{2,1,0:T(8,128)(2,1)S(1)} collective-permute-done((bf16[4,128,256]{2,1,0:T(8,128)(2,1)S(1)}, bf16[4,128,256]{2,1,0:T(8,128)(2,1)S(1)}, u32[]{:S(2)}, u32[]{:S(2)}) %collective-permute-start.32) | collective-permute-done | bytes 262176 | tf_op jit(solution)/shard_map/ppermute | solution.py:74
  94.6 5.9 %combine.3 = bf16[256,1024]{1,0:T(8,128)(2,1)} custom-call(s32[5]{0:T(128)S(1)} %get-tuple-element.63.place_ref, s32[8,1,256]{2,1,0:T(1,128)S(1)} %get-tuple-element.47.slot_ref, f32[8,1,256]{2,1,0:T(1,128)S(1)} %get-tuple-element.53.gate_ref, bf16[4,128,256]{2,1,0:T(8,128)(2,1)S(1)} %hidden.3.refs_0_, ...), custom_call_target="tpu_custom_call" | custom-call | tf_op jit(solution)/shard_map/combine/pallas_call | solution.py:346
  100.5 4.9 %all-to-all-start = ((bf16[16,16,1024]{2,1,0:T(8,128)(2,1)}), bf16[16,16,1024]{2,1,0:T(8,128)(2,1)S(1)}, u32[]{:S(2)}, u32[]{:S(2)}) async-start(bf16[16,16,1024]{2,1,0:T(8,128)(2,1)} %bitcast.19), calls=%async_computation | async-start | bytes 1048576 | tf_op jit(solution)/shard_map/all_to_all | solution.py:479
  106.0 13.7 %all-to-all-done = bf16[16,16,1024]{2,1,0:T(8,128)(2,1)S(1)} async-done(((bf16[16,16,1024]{2,1,0:T(8,128)(2,1)}), bf16[16,16,1024]{2,1,0:T(8,128)(2,1)S(1)}, u32[]{:S(2)}, u32[]{:S(2)}) %all-to-all-start) | async-done | bytes 524320 | tf_op jit(solution)/shard_map/all_to_all | solution.py:479
  (62 shorter events, 14.5 us)
Async XLA Ops:
  3.6 9.9 %collective-permute-start.2 = (bf16[64,1024]{1,0:T(8,128)(2,1)}, bf16[64,1024]{1,0:T(8,128)(2,1)S(1)}, u32[]{:S(2)}, u32[]{:S(2)}) collective-permute-start(bf16[64,1024]{1,0:T(8,128)(2,1)} %attend.1), channel_id=1, source_target_pairs={{12,0},{0,4},{4,8},{8,12},{13,1},{1,5},{5,9},{9,13},{14,2},{2,6},{... | collective-permute-start | bytes 393224 | tf_op jit(solution)/shard_map/ppermute | solution.py:54
  6.6 11.4 %collective-permute-start.1 = (bf16[64,1024]{1,0:T(8,128)(2,1)}, bf16[64,1024]{1,0:T(8,128)(2,1)S(1)}, u32[]{:S(2)}, u32[]{:S(2)}) collective-permute-start(bf16[64,1024]{1,0:T(8,128)(2,1)} %attend.1), channel_id=1, source_target_pairs={{8,0},{12,4},{0,8},{4,12},{9,1},{13,5},{1,9},{5,13},{10,2},{14,6},... | collective-permute-start | bytes 393224 | tf_op jit(solution)/shard_map/ppermute | solution.py:54
  9.2 8.9 %collective-permute-start = (bf16[64,1024]{1,0:T(8,128)(2,1)}, bf16[64,1024]{1,0:T(8,128)(2,1)S(1)}, u32[]{:S(2)}, u32[]{:S(2)}) collective-permute-start(bf16[64,1024]{1,0:T(8,128)(2,1)} %attend.1), channel_id=1, source_target_pairs={{4,0},{8,4},{12,8},{0,12},{5,1},{9,5},{13,9},{1,13},{6,2},{10,6},{... | collective-permute-start | bytes 393224 | tf_op jit(solution)/shard_map/ppermute | solution.py:54
  21.9 15.1 %collective-permute-start.3 = (bf16[4,16,1024]{2,1,0:T(8,128)(2,1)S(1)}, bf16[4,16,1024]{2,1,0:T(8,128)(2,1)S(1)}, u32[]{:S(2)}, u32[]{:S(2)}) collective-permute-start(bf16[4,16,1024]{2,1,0:T(8,128)(2,1)S(1)} %get-tuple-element.39), channel_id=1, source_target_pairs={{0,1},{1,0},{2,3},{3,2},{4,5},{5,4},{6,7},{7,6},{8,9},{9,8},{10,11... | collective-permute-start | bytes 393224 | tf_op jit(solution)/shard_map/ppermute | solution.py:74
  22.0 15.1 %collective-permute-start.4 = (bf16[4,16,1024]{2,1,0:T(8,128)(2,1)S(1)}, bf16[4,16,1024]{2,1,0:T(8,128)(2,1)S(1)}, u32[]{:S(2)}, u32[]{:S(2)}) collective-permute-start(bf16[4,16,1024]{2,1,0:T(8,128)(2,1)S(1)} %get-tuple-element.40), channel_id=1, source_target_pairs={{0,2},{1,3},{2,0},{3,1},{4,6},{5,7},{6,4},{7,5},{8,10},{9,11},{10,... | collective-permute-start | bytes 393224 | tf_op jit(solution)/shard_map/ppermute | solution.py:74
  23.5 13.5 %collective-permute-start.5 = (bf16[4,16,1024]{2,1,0:T(8,128)(2,1)S(1)}, bf16[4,16,1024]{2,1,0:T(8,128)(2,1)S(1)}, u32[]{:S(2)}, u32[]{:S(2)}) collective-permute-start(bf16[4,16,1024]{2,1,0:T(8,128)(2,1)S(1)} %get-tuple-element.41), channel_id=1, source_target_pairs={{0,3},{1,2},{2,1},{3,0},{4,7},{5,6},{6,5},{7,4},{8,11},{9,10},{10,... | collective-permute-start | bytes 393224 | tf_op jit(solution)/shard_map/ppermute | solution.py:74
  24.8 6.0 %collective-permute-start.6 = (bf16[16,1024]{1,0:T(8,128)(2,1)S(1)}, bf16[16,1024]{1,0:T(8,128)(2,1)S(1)}, u32[]{:S(2)}, u32[]{:S(2)}) collective-permute-start(bf16[16,1024]{1,0:T(8,128)(2,1)S(1)} %get-tuple-element.42), channel_id=1, source_target_pairs={{4,0},{8,4},{12,8},{0,12},{5,1},{9,5},{13,9},{1,13},{6,2},{10,6},{... | collective-permute-start | bytes 98312 | tf_op jit(solution)/shard_map/ppermute | solution.py:68
  29.2 4.8 %collective-permute-start.7 = (bf16[16,1024]{1,0:T(8,128)(2,1)S(1)}, bf16[16,1024]{1,0:T(8,128)(2,1)S(1)}, u32[]{:S(2)}, u32[]{:S(2)}) collective-permute-start(bf16[16,1024]{1,0:T(8,128)(2,1)S(1)} %get-tuple-element.43), channel_id=1, source_target_pairs={{8,0},{12,4},{0,8},{4,12},{9,1},{13,5},{1,9},{5,13},{10,2},{14,6},... | collective-permute-start | bytes 98312 | tf_op jit(solution)/shard_map/ppermute | solution.py:68
  30.8 6.2 %collective-permute-start.8 = (bf16[16,1024]{1,0:T(8,128)(2,1)S(1)}, bf16[16,1024]{1,0:T(8,128)(2,1)S(1)}, u32[]{:S(2)}, u32[]{:S(2)}) collective-permute-start(bf16[16,1024]{1,0:T(8,128)(2,1)S(1)} %get-tuple-element.44), channel_id=1, source_target_pairs={{12,0},{0,4},{4,8},{8,12},{13,1},{1,5},{5,9},{9,13},{14,2},{2,6},{... | collective-permute-start | bytes 98312 | tf_op jit(solution)/shard_map/ppermute | solution.py:68
  37.7 5.9 %collective-permute-start.14 = (f32[16,64]{1,0:T(8,128)S(1)}, f32[16,64]{1,0:T(8,128)S(1)}, u32[]{:S(2)}, u32[]{:S(2)}) collective-permute-start(f32[16,64]{1,0:T(8,128)S(1)} %pad_maximum_fusion.1), channel_id=1, source_target_pairs={{12,0},{0,4},{4,8},{8,12},{13,1},{1,5},{5,9},{9,13},{14,2},{2,6},{... | collective-permute-start | bytes 12296 | tf_op jit(solution)/shard_map/ppermute | solution.py:54
  37.7 8.8 %collective-permute-start.13 = (f32[16,64]{1,0:T(8,128)S(1)}, f32[16,64]{1,0:T(8,128)S(1)}, u32[]{:S(2)}, u32[]{:S(2)}) collective-permute-start(f32[16,64]{1,0:T(8,128)S(1)} %pad_maximum_fusion.1), channel_id=1, source_target_pairs={{8,0},{12,4},{0,8},{4,12},{9,1},{13,5},{1,9},{5,13},{10,2},{14,6},... | collective-permute-start | bytes 12296 | tf_op jit(solution)/shard_map/ppermute | solution.py:54
  40.3 7.6 %collective-permute-start.12 = (f32[16,64]{1,0:T(8,128)S(1)}, f32[16,64]{1,0:T(8,128)S(1)}, u32[]{:S(2)}, u32[]{:S(2)}) collective-permute-start(f32[16,64]{1,0:T(8,128)S(1)} %pad_maximum_fusion.1), channel_id=1, source_target_pairs={{4,0},{8,4},{12,8},{0,12},{5,1},{9,5},{13,9},{1,13},{6,2},{10,6},{... | collective-permute-start | bytes 12296 | tf_op jit(solution)/shard_map/ppermute | solution.py:54
  41.5 7.9 %collective-permute-start.11 = (bf16[64,1024]{1,0:T(8,128)(2,1)S(1)}, bf16[64,1024]{1,0:T(8,128)(2,1)S(1)}, u32[]{:S(2)}, u32[]{:S(2)}) collective-permute-start(bf16[64,1024]{1,0:T(8,128)(2,1)S(1)} %bitcast.33), channel_id=1, source_target_pairs={{12,0},{0,4},{4,8},{8,12},{13,1},{1,5},{5,9},{9,13},{14,2},{2,6},{... | collective-permute-start | bytes 393224 | tf_op jit(solution)/shard_map/ppermute | solution.py:54
  42.3 10.1 %collective-permute-start.10 = (bf16[64,1024]{1,0:T(8,128)(2,1)S(1)}, bf16[64,1024]{1,0:T(8,128)(2,1)S(1)}, u32[]{:S(2)}, u32[]{:S(2)}) collective-permute-start(bf16[64,1024]{1,0:T(8,128)(2,1)S(1)} %bitcast.34), channel_id=1, source_target_pairs={{8,0},{12,4},{0,8},{4,12},{9,1},{13,5},{1,9},{5,13},{10,2},{14,6},... | collective-permute-start | bytes 393224 | tf_op jit(solution)/shard_map/ppermute | solution.py:54
  43.6 8.9 %collective-permute-start.9 = (bf16[64,1024]{1,0:T(8,128)(2,1)S(1)}, bf16[64,1024]{1,0:T(8,128)(2,1)S(1)}, u32[]{:S(2)}, u32[]{:S(2)}) collective-permute-start(bf16[64,1024]{1,0:T(8,128)(2,1)S(1)} %bitcast.35), channel_id=1, source_target_pairs={{4,0},{8,4},{12,8},{0,12},{5,1},{9,5},{13,9},{1,13},{6,2},{10,6},{... | collective-permute-start | bytes 393224 | tf_op jit(solution)/shard_map/ppermute | solution.py:54
  46.5 7.4 %collective-permute-start.16 = (bf16[1,64,1024]{2,1,0:T(8,128)(2,1)S(1)}, bf16[1,64,1024]{2,1,0:T(8,128)(2,1)S(1)}, u32[]{:S(2)}, u32[]{:S(2)}) collective-permute-start(bf16[1,64,1024]{2,1,0:T(8,128)(2,1)S(1)} %bitcast.36), channel_id=1, source_target_pairs={{0,2},{1,3},{2,0},{3,1},{4,6},{5,7},{6,4},{7,5},{8,10},{9,11},{10,... | collective-permute-start | bytes 393224 | tf_op jit(solution)/shard_map/ppermute | solution.py:74
  48.0 6.2 %collective-permute-start.15 = (bf16[1,64,1024]{2,1,0:T(8,128)(2,1)S(1)}, bf16[1,64,1024]{2,1,0:T(8,128)(2,1)S(1)}, u32[]{:S(2)}, u32[]{:S(2)}) collective-permute-start(bf16[1,64,1024]{2,1,0:T(8,128)(2,1)S(1)} %bitcast.37), channel_id=1, source_target_pairs={{0,1},{1,0},{2,3},{3,2},{4,5},{5,4},{6,7},{7,6},{8,9},{9,8},{10,11... | collective-permute-start | bytes 393224 | tf_op jit(solution)/shard_map/ppermute | solution.py:74
  49.4 5.3 %collective-permute-start.25 = (bf16[1,64,1024]{2,1,0:T(8,128)(2,1)S(1)}, bf16[1,64,1024]{2,1,0:T(8,128)(2,1)S(1)}, u32[]{:S(2)}, u32[]{:S(2)}) collective-permute-start(bf16[1,64,1024]{2,1,0:T(8,128)(2,1)S(1)} %bitcast.41), channel_id=1, source_target_pairs={{0,2},{1,3},{2,0},{3,1},{4,6},{5,7},{6,4},{7,5},{8,10},{9,11},{10,... | collective-permute-start | bytes 393224 | tf_op jit(solution)/shard_map/ppermute | solution.py:74
  52.5 2.3 %collective-permute-start.24 = (bf16[1,64,1024]{2,1,0:T(8,128)(2,1)S(1)}, bf16[1,64,1024]{2,1,0:T(8,128)(2,1)S(1)}, u32[]{:S(2)}, u32[]{:S(2)}) collective-permute-start(bf16[1,64,1024]{2,1,0:T(8,128)(2,1)S(1)} %bitcast.42), channel_id=1, source_target_pairs={{0,1},{1,0},{2,3},{3,2},{4,5},{5,4},{6,7},{7,6},{8,9},{9,8},{10,11... | collective-permute-start | bytes 393224 | tf_op jit(solution)/shard_map/ppermute | solution.py:74
  52.5 6.4 %collective-permute-start.22 = (bf16[1,64,1024]{2,1,0:T(8,128)(2,1)S(1)}, bf16[1,64,1024]{2,1,0:T(8,128)(2,1)S(1)}, u32[]{:S(2)}, u32[]{:S(2)}) collective-permute-start(bf16[1,64,1024]{2,1,0:T(8,128)(2,1)S(1)} %bitcast.46), channel_id=1, source_target_pairs={{0,2},{1,3},{2,0},{3,1},{4,6},{5,7},{6,4},{7,5},{8,10},{9,11},{10,... | collective-permute-start | bytes 393224 | tf_op jit(solution)/shard_map/ppermute | solution.py:74
  53.9 4.9 %collective-permute-start.21 = (bf16[1,64,1024]{2,1,0:T(8,128)(2,1)S(1)}, bf16[1,64,1024]{2,1,0:T(8,128)(2,1)S(1)}, u32[]{:S(2)}, u32[]{:S(2)}) collective-permute-start(bf16[1,64,1024]{2,1,0:T(8,128)(2,1)S(1)} %bitcast.47), channel_id=1, source_target_pairs={{0,1},{1,0},{2,3},{3,2},{4,5},{5,4},{6,7},{7,6},{8,9},{9,8},{10,11... | collective-permute-start | bytes 393224 | tf_op jit(solution)/shard_map/ppermute | solution.py:74
  54.1 7.0 %collective-permute-start.19 = (bf16[1,64,1024]{2,1,0:T(8,128)(2,1)S(1)}, bf16[1,64,1024]{2,1,0:T(8,128)(2,1)S(1)}, u32[]{:S(2)}, u32[]{:S(2)}) collective-permute-start(bf16[1,64,1024]{2,1,0:T(8,128)(2,1)S(1)} %bitcast.51), channel_id=1, source_target_pairs={{0,2},{1,3},{2,0},{3,1},{4,6},{5,7},{6,4},{7,5},{8,10},{9,11},{10,... | collective-permute-start | bytes 393224 | tf_op jit(solution)/shard_map/ppermute | solution.py:74
  54.7 7.3 %collective-permute-start.18 = (bf16[1,64,1024]{2,1,0:T(8,128)(2,1)S(1)}, bf16[1,64,1024]{2,1,0:T(8,128)(2,1)S(1)}, u32[]{:S(2)}, u32[]{:S(2)}) collective-permute-start(bf16[1,64,1024]{2,1,0:T(8,128)(2,1)S(1)} %bitcast.52), channel_id=1, source_target_pairs={{0,1},{1,0},{2,3},{3,2},{4,5},{5,4},{6,7},{7,6},{8,9},{9,8},{10,11... | collective-permute-start | bytes 393224 | tf_op jit(solution)/shard_map/ppermute | solution.py:74
  54.7 7.2 %collective-permute-start.17 = (bf16[1,64,1024]{2,1,0:T(8,128)(2,1)S(1)}, bf16[1,64,1024]{2,1,0:T(8,128)(2,1)S(1)}, u32[]{:S(2)}, u32[]{:S(2)}) collective-permute-start(bf16[1,64,1024]{2,1,0:T(8,128)(2,1)S(1)} %collective-permute-done.16.refs_2_), channel_id=1, source_target_pairs={{0,1},{1,0},{2,3},{3,2},{4,5},{5,4},{6,7},{7,6},{8,9},{9,8},{10,11... | collective-permute-start | bytes 393224 | tf_op jit(solution)/shard_map/ppermute | solution.py:74
  58.8 3.2 %collective-permute-start.26 = (bf16[1,64,1024]{2,1,0:T(8,128)(2,1)S(1)}, bf16[1,64,1024]{2,1,0:T(8,128)(2,1)S(1)}, u32[]{:S(2)}, u32[]{:S(2)}) collective-permute-start(bf16[1,64,1024]{2,1,0:T(8,128)(2,1)S(1)} %collective-permute-done.25.refs_14_), channel_id=1, source_target_pairs={{0,1},{1,0},{2,3},{3,2},{4,5},{5,4},{6,7},{7,6},{8,9},{9,8},{10,11... | collective-permute-start | bytes 393224 | tf_op jit(solution)/shard_map/ppermute | solution.py:74
  58.8 3.2 %collective-permute-start.23 = (bf16[1,64,1024]{2,1,0:T(8,128)(2,1)S(1)}, bf16[1,64,1024]{2,1,0:T(8,128)(2,1)S(1)}, u32[]{:S(2)}, u32[]{:S(2)}) collective-permute-start(bf16[1,64,1024]{2,1,0:T(8,128)(2,1)S(1)} %collective-permute-done.22.refs_10_), channel_id=1, source_target_pairs={{0,1},{1,0},{2,3},{3,2},{4,5},{5,4},{6,7},{7,6},{8,9},{9,8},{10,11... | collective-permute-start | bytes 393224 | tf_op jit(solution)/shard_map/ppermute | solution.py:74
  73.0 11.1 %collective-permute-start.27 = (bf16[4,128,256]{2,1,0:T(8,128)(2,1)S(1)}, bf16[4,128,256]{2,1,0:T(8,128)(2,1)S(1)}, u32[]{:S(2)}, u32[]{:S(2)}) collective-permute-start(bf16[4,128,256]{2,1,0:T(8,128)(2,1)S(1)} %get-tuple-element.54.refs_0_), channel_id=1, source_target_pairs={{0,2},{1,3},{2,0},{3,1},{4,6},{5,7},{6,4},{7,5},{8,10},{9,11},{10,... | collective-permute-start | bytes 786440 | tf_op jit(solution)/shard_map/ppermute | solution.py:74
  74.5 10.8 %collective-permute-start.30 = (bf16[4,128,256]{2,1,0:T(8,128)(2,1)S(1)}, bf16[4,128,256]{2,1,0:T(8,128)(2,1)S(1)}, u32[]{:S(2)}, u32[]{:S(2)}) collective-permute-start(bf16[4,128,256]{2,1,0:T(8,128)(2,1)S(1)} %get-tuple-element.54.refs_0_), channel_id=1, source_target_pairs={{0,1},{1,0},{2,3},{3,2},{4,5},{5,4},{6,7},{7,6},{8,9},{9,8},{10,11... | collective-permute-start | bytes 786440 | tf_op jit(solution)/shard_map/ppermute | solution.py:74
  84.2 1.7 %collective-permute-start.31 = (bf16[4,128,256]{2,1,0:T(8,128)(2,1)S(1)}, bf16[4,128,256]{2,1,0:T(8,128)(2,1)S(1)}, u32[]{:S(2)}, u32[]{:S(2)}) collective-permute-start(bf16[4,128,256]{2,1,0:T(8,128)(2,1)S(1)} %collective-permute-done.27.refs_2_), channel_id=1, source_target_pairs={{0,1},{1,0},{2,3},{3,2},{4,5},{5,4},{6,7},{7,6},{8,9},{9,8},{10,11... | collective-permute-start | bytes 786440 | tf_op jit(solution)/shard_map/ppermute | solution.py:74
  84.7 8.3 %collective-permute-start.29 = (bf16[4,128,256]{2,1,0:T(8,128)(2,1)S(1)}, bf16[4,128,256]{2,1,0:T(8,128)(2,1)S(1)}, u32[]{:S(2)}, u32[]{:S(2)}) collective-permute-start(bf16[4,128,256]{2,1,0:T(8,128)(2,1)S(1)} %hidden.3.refs_0_), channel_id=1, source_target_pairs={{0,2},{1,3},{2,0},{3,1},{4,6},{5,7},{6,4},{7,5},{8,10},{9,11},{10,... | collective-permute-start | bytes 786440 | tf_op jit(solution)/shard_map/ppermute | solution.py:74
  85.3 7.7 %collective-permute-start.28 = (bf16[4,128,256]{2,1,0:T(8,128)(2,1)S(1)}, bf16[4,128,256]{2,1,0:T(8,128)(2,1)S(1)}, u32[]{:S(2)}, u32[]{:S(2)}) collective-permute-start(bf16[4,128,256]{2,1,0:T(8,128)(2,1)S(1)} %hidden.3.refs_0_), channel_id=1, source_target_pairs={{0,1},{1,0},{2,3},{3,2},{4,5},{5,4},{6,7},{7,6},{8,9},{9,8},{10,11... | collective-permute-start | bytes 786440 | tf_op jit(solution)/shard_map/ppermute | solution.py:74
  100.5 19.2 %all-to-all-start = ((bf16[16,16,1024]{2,1,0:T(8,128)(2,1)}), bf16[16,16,1024]{2,1,0:T(8,128)(2,1)S(1)}, u32[]{:S(2)}, u32[]{:S(2)}) async-start(bf16[16,16,1024]{2,1,0:T(8,128)(2,1)} %bitcast.19), calls=%async_computation | async-start | bytes 1048576 | tf_op jit(solution)/shard_map/all_to_all | solution.py:479
  (5 other events, 19.7 us)
